TPU v7x, 512 devices: a whole 4x8x8 slice. The times are simulated.
512 devices in a mesh: grp: 8 (over y), tm: 64 (over z, x, core).
Axes of the slice: x: 4, y: 8, z: 8, core: 2. Of those that a mesh axis runs over, the one named last changes fastest.
Arguments:
- audio_rows: bfloat16 [131072, 1024], P(('grp', 'tm')), may hold values from -6 to 6
- routing: int32 [131072, 1], P(('grp', 'tm')), may hold values from 0 to 63; in each aligned block of 256 rows (0 to 255, 256 to 511, ...) at most 8 rows name the same one
- row_band: int32 [131072], P(('grp', 'tm')), may hold values from 0 to 3
- block_band: int32 [512], P(('grp', 'tm')), may hold values from 0 to 3
- latents: bfloat16 [65536, 1024], P(('grp', 'tm')), may hold values from -480 to 480
- kv_weight: bfloat16 [1024, 2048], P('tm'), may hold values from -0.1875 to 0.1875
- null_key: float32 [1024], replicated, may hold values from -6 to 6
- null_value: float32 [1024], replicated, may hold values from -6 to 6
- out_weight: bfloat16 [1024, 1024], replicated, may hold values from -0.1875 to 0.1875
- mlp_gain: float32 [1024], replicated, may hold values from 0.25 to 1.75
- up_weight: bfloat16 [1024, 8192], P('tm', 'grp'), may hold values from -0.1875 to 0.1875
- down_weight: bfloat16 [8192, 1024], P('grp', 'tm'), may hold values from -0.25 to 0.25
Outputs:
- mixed: bfloat16 [65536, 1024], P('tm', 'grp')
Inputs may be any that keep to these rules, and one draw needn't show every extreme that they name: `routing`: among the rows of one device no window is named by more than 8 rows, and in some devices' rows one window is named by exactly 8.
All inputs are finite; a program needn't handle non-finite values.
Results may differ from a plain program's by a relative error of at most 0.015.
Values may be sent and summed in bfloat16 or wider, within the bound.
No kernel may reach another device: no remote copies, remote signals or barrier semaphores. Data moves between devices by JAX's collectives and lax.ppermute only.
A program may use at most 64 MiB of HBM per device.

v0:
```python
import jax
import jax.numpy as jnp
from jax import lax
from jax.sharding import PartitionSpec as P

HD = 128


def attend(queries, kv_slots, usable, null_key, null_value):
    count = queries.shape[0]
    slots = kv_slots.shape[0]
    width = queries.shape[1]
    heads = width // HD
    scale = 1.0 / float(HD) ** 0.5
    query = queries.reshape(count, heads, HD)
    keyset = kv_slots[:, :width].reshape(slots, heads, HD)
    valset = kv_slots[:, width:].reshape(slots, heads, HD)
    scores = jnp.einsum("lhd,shd->hls", query, keyset, preferred_element_type=jnp.float32) * scale
    null_scores = (
        jnp.einsum("lhd,hd->hl", query.astype(jnp.float32), null_key.reshape(heads, HD)) * scale
    )
    masked = jnp.where(usable[None, None, :], scores, -1e30)
    highest = jnp.maximum(jnp.max(masked, axis=-1), null_scores)
    expo = jnp.where(usable[None, None, :], jnp.exp(masked - highest[:, :, None]), 0.0)
    null_expo = jnp.exp(null_scores - highest)
    denom = jnp.sum(expo, axis=-1) + null_expo
    weights = (expo / denom[:, :, None]).astype(jnp.bfloat16)
    null_weights = (null_expo / denom).astype(jnp.bfloat16)
    summed = jnp.einsum("hls,shd->lhd", weights, valset, preferred_element_type=jnp.float32)
    summed = (
        summed
        + jnp.transpose(null_weights.astype(jnp.float32))[:, :, None]
        * null_value.reshape(heads, HD)[None, :, :]
    )
    return summed.reshape(count, width).astype(jnp.bfloat16)


def local(
    audio_rows,
    routing,
    row_band,
    block_band,
    latents,
    kv_weight,
    null_key,
    null_value,
    out_weight,
    mlp_gain,
    up_weight,
    down_weight,
):
    local_rows = audio_rows.shape[0]
    owners = lax.axis_size("tm")
    capacity = max(2, 2 * local_rows // owners)
    destination = routing[:, 0]
    onehot = (destination[:, None] == jnp.arange(owners, dtype=jnp.int32)[None, :]).astype(
        jnp.int32
    )
    slot_index = jnp.sum((jnp.cumsum(onehot, axis=0) - onehot) * onehot, axis=1)
    band_send = (
        jnp.full((owners, capacity), -4, jnp.int32).at[destination, slot_index].set(row_band)
    )
    payload = (
        jnp.zeros((owners, capacity, audio_rows.shape[1]), jnp.bfloat16)
        .at[destination, slot_index]
        .set(audio_rows)
    )
    frame_recv, band_recv = (
        lax.all_to_all(payload, "tm", split_axis=0, concat_axis=0, tiled=True),
        lax.all_to_all(band_send, "tm", split_axis=0, concat_axis=0, tiled=True),
    )
    frame_slots = frame_recv.reshape(owners * capacity, audio_rows.shape[1])
    kv_whole = lax.all_gather(kv_weight, "tm", axis=0, tiled=True)
    kv_slots = jnp.dot(frame_slots, kv_whole, preferred_element_type=jnp.float32).astype(
        jnp.bfloat16
    )
    usable = jnp.abs(band_recv.reshape(-1) - block_band[0]) <= 1
    attended = attend(latents, kv_slots, usable, null_key, null_value)
    joined = (
        latents.astype(jnp.float32)
        + jnp.dot(attended, out_weight, preferred_element_type=jnp.float32)
    ).astype(jnp.bfloat16)
    window = lax.all_gather(joined, "grp", axis=0, tiled=True)
    values = window.astype(jnp.float32)
    center = values - jnp.mean(values, axis=-1, keepdims=True)
    spread = jnp.mean(center * center, axis=-1, keepdims=True)
    normed = (center * lax.rsqrt(spread + 1e-05) * mlp_gain).astype(jnp.bfloat16)
    up_whole = lax.all_gather(up_weight, "tm", axis=0, tiled=True)
    hidden = jax.nn.gelu(jnp.dot(normed, up_whole, preferred_element_type=jnp.float32)).astype(
        jnp.bfloat16
    )
    down_whole = lax.all_gather(down_weight, "tm", axis=1, tiled=True)
    partial_terms = jnp.dot(hidden, down_whole, preferred_element_type=jnp.float32)
    summed = lax.psum_scatter(
        partial_terms.astype(jnp.bfloat16), "grp", scatter_dimension=1, tiled=True
    ).astype(jnp.float32)
    columns = summed.shape[1]
    residual = lax.dynamic_slice_in_dim(window, lax.axis_index("grp") * columns, columns, 1)
    return (residual.astype(jnp.float32) + summed).astype(jnp.bfloat16)


def solution(mesh):
    return jax.shard_map(
        local,
        mesh=mesh,
        in_specs=(
            P(("grp", "tm"), None),
            P(("grp", "tm"), None),
            P(("grp", "tm")),
            P(("grp", "tm")),
            P(("grp", "tm"), None),
            P("tm", None),
            P(),
            P(),
            P(),
            P(),
            P("tm", "grp"),
            P("grp", "tm"),
        ),
        out_specs=P("tm", "grp"),
        check_vma=False,
    )
```

profile of v0, /device:TPU:4, one launch (start us, length us, event | category | flops | bytes accessed | tf_op | source)
XLA Modules:
  0.0 409.4 jit_solution(6860306548943538803)
XLA Ops:
  6.5 0.0 copy-start
  6.5 0.0 all-gather.5.cloned.1.call-start
  6.5 0.7 all-gather.5.cloned.1.call-update
  7.3 0.7 fusion.51
  8.0 0.6 reduce-window.6
  8.6 0.2 slice_reduce_fusion
  8.8 0.8 fusion.50
  9.6 0.7 or_select_fusion
  10.3 21.2 %scatter_fusion.1 = s32[64,8]{0,1:T(8,128)S(1)} fusion(s32[64,8]{0,1:T(8,128)S(1)} %broadcast_in_dim.40, s32[256]{0:T(256)S(1)} %bitcast.106, s32[256]{0:T(256)} %param.14), kind=kCustom, calls=%fused_computation.1 | custom fusion | bytes 5120 | tf_op jit(solution)/shard_map/scatter | solution.py:61
  31.6 0.7 copy.24
  32.3 13.8 %all-to-all-start.1 = ((s32[64,1,8]{2,1,0:T(1,128)}), s32[64,1,8]{2,1,0:T(1,128)S(1)}, u32[]{:S(2)}, u32[]{:S(2)}) async-start(s32[64,1,8]{2,1,0:T(1,128)} %copy.24), calls=%async_computation.1 | async-start | bytes 65536 | tf_op jit(solution)/shard_map/all_to_all | solution.py:70
  46.1 1.1 broadcast_in_dim.39
  47.2 0.0 copy-done.3
  47.2 36.2 %scatter_fusion = bf16[64,8,1024]{2,1,0:T(8,128)(2,1)} fusion(bf16[64,8,1024]{2,1,0:T(8,128)(2,1)} %broadcast_in_dim.39, s32[256]{0:T(256)S(1)} %bitcast.107, bf16[256,1024]{1,0:T(8,128)(2,1)S(1)} %copy-done.3), kind=kCustom, calls=%fused_computation | custom fusion | bytes 1574912 | tf_op jit(solution)/shard_map/scatter | solution.py:66
  83.4 0.0 all-to-all-done.1
  83.4 10.6 %all-to-all-start = ((bf16[64,8,1024]{2,1,0:T(8,128)(2,1)}), bf16[64,8,1024]{2,1,0:T(8,128)(2,1)S(1)}, u32[]{:S(2)}, u32[]{:S(2)}) async-start(bf16[64,8,1024]{2,1,0:T(8,128)(2,1)} %scatter_fusion), calls=%async_computation | async-start | bytes 2097152 | tf_op jit(solution)/shard_map/all_to_all | solution.py:69
  94.0 0.0 all-gather.7.cloned.1.call-start
  94.7 0.2 fusion.43
  95.0 0.2 compare_reduce_fusion
  95.1 0.1 le.15
  95.2 27.6 %all-to-all-done = bf16[64,8,1024]{2,1,0:T(8,128)(2,1)S(1)} async-done(((bf16[64,8,1024]{2,1,0:T(8,128)(2,1)}), bf16[64,8,1024]{2,1,0:T(8,128)(2,1)S(1)}, u32[]{:S(2)}, u32[]{:S(2)}) %all-to-all-start) | async-done | bytes 1048608 | tf_op jit(solution)/shard_map/all_to_all | solution.py:69
  122.8 4.5 %convolution_convert_fusion = bf16[512,2048]{1,0:T(8,128)(2,1)S(1)} fusion(bf16[1024,2048]{1,0:T(8,128)(2,1)} %all-gather.5.cloned.1.call-done, bf16[64,8,1024]{2,1,0:T(8,128)(2,1)S(1)} %all-to-all-done), kind=kOutput, calls=%fused_computation.18 | convolution fusion | flops 2148532224 | bytes 7340032 | tf_op jit(solution)/shard_map/dot_general | solution.py:74
  127.3 0.2 slice_bitcast_fusion
  127.5 0.5 bitcast_reduce_fusion
  128.1 1.3 copy-done.2
  129.4 0.6 fusion.29
  130.1 1.3 copy.32
  131.4 2.9 fusion.31
  134.3 1.2 fusion.32
  135.5 0.0 all-gather.7.cloned.1.call-update
  135.5 0.0 all-gather.11.cloned.1.call-start
  135.6 0.7 all-gather.11.cloned.1.call-update
  136.3 0.0 all-gather.9.cloned.1.call-start
  136.3 0.5 all-gather.9.cloned.1.call-update
  136.8 0.0 copy-start.7
  136.8 0.2 reduce-scatter.4.cloned.1.call-start
  137.1 38.1 %all-gather.7.cloned.1.call-done = bf16[1024,1024]{1,0:T(8,128)(2,1)} async-done(((bf16[128,1024]{1,0:T(8,128)(2,1)}), bf16[1024,1024]{1,0:T(8,128)(2,1)}) %all-gather.7.cloned.1.call-update) | async-done | bytes 2097168 | tf_op jit(solution)/shard_map/all_gather | solution.py:83
  175.2 2.1 convert_reduce_fusion
  177.3 0.1 copy-done.1
  177.4 0.7 fusion.2
  178.1 81.9 %all-gather.11.cloned.1.call-done = bf16[1024,1024]{0,1:T(8,128)(2,1)} async-done(((bf16[1024,16]{0,1:T(8,128)(2,1)}), bf16[1024,1024]{0,1:T(8,128)(2,1)}) %all-gather.11.cloned.1.call-update) | async-done | bytes 2097168 | tf_op jit(solution)/shard_map/all_gather | solution.py:92
  260.0 83.9 %all-gather.9.cloned.1.call-done = bf16[1024,1024]{1,0:T(8,128)(2,1)} async-done(((bf16[16,1024]{1,0:T(8,128)(2,1)}), bf16[1024,1024]{1,0:T(8,128)(2,1)}) %all-gather.9.cloned.1.call-update) | async-done | bytes 2097168 | tf_op jit(solution)/shard_map/all_gather | solution.py:88
  343.9 8.8 %fusion.26 = bf16[1024,1024]{1,0:T(8,128)(2,1)} fusion(bf16[1024,1024]{0,1:T(8,128)(2,1)} %all-gather.11.cloned.1.call-done, bf16[1024,1024]{1,0:T(8,128)(2,1)} %all-gather.9.cloned.1.call-done, bf16[1024,1024]{1,0:T(8,128)(2,1)} %all-gather.7.cloned.1.call-done, f32[1024]{0:T(1024)S(1)} %copy-done.7, f32[1024]{0:T(1024)S(1)} %add_rsqrt_fusion, ...), kind=kOutput, calls=%fused_computation.34 | convolution fusion | flops 4310695936 | bytes 8400896 | tf_op jit(solution)/shard_map/dot_general | solution.py:93
  352.7 3.9 copy.33
  356.6 0.0 reduce-scatter.4.cloned.1.call-update
  356.7 43.3 %reduce-scatter.4.cloned.1.call-done = bf16[128,1024]{1,0:T(8,128)(2,1)} async-done(((bf16[1024,1024]{1,0:T(8,128)(2,1)}), bf16[128,1024]{1,0:T(8,128)(2,1)}) %reduce-scatter.4.cloned.1.call-update) | async-done | bytes 262160
  400.0 1.1 copy.34
  401.1 1.7 add_convert_fusion
  (20 shorter events, 0.1 us)
Async XLA Ops:
  6.5 127.8 %copy-start = (bf16[1024,1024]{1,0:T(8,128)(2,1)S(1)}, bf16[1024,1024]{1,0:T(8,128)(2,1)}, u32[]{:S(2)}) copy-start(bf16[1024,1024]{1,0:T(8,128)(2,1)} %param.20) | copy-start | bytes 6291460
  6.5 40.7 %copy-start.3 = (bf16[256,1024]{1,0:T(8,128)(2,1)S(1)}, bf16[256,1024]{1,0:T(8,128)(2,1)}, u32[]{:S(2)}) copy-start(bf16[256,1024]{1,0:T(8,128)(2,1)} %param.12) | copy-start | bytes 1572868
  6.5 116.3 %all-gather.5.cloned.1.call-start = ((), (), s32[]{:S(2)}) async-start(), calls=%async_computation.3 | async-start | bytes 4259840 | tf_op jit(solution)/shard_map/all_gather | solution.py:73
  32.3 51.1 %all-to-all-start.1 = ((s32[64,1,8]{2,1,0:T(1,128)}), s32[64,1,8]{2,1,0:T(1,128)S(1)}, u32[]{:S(2)}, u32[]{:S(2)}) async-start(s32[64,1,8]{2,1,0:T(1,128)} %copy.24), calls=%async_computation.1 | async-start | bytes 65536 | tf_op jit(solution)/shard_map/all_to_all | solution.py:70
  83.4 11.3 %copy-start.4 = (bf16[128,1024]{1,0:T(8,128)(2,1)S(1)}, bf16[128,1024]{1,0:T(8,128)(2,1)}, u32[]{:S(2)}) copy-start(bf16[128,1024]{1,0:T(8,128)(2,1)} %param.16) | copy-start | bytes 786436
  83.4 11.3 %copy-start.5 = (f32[1024]{0:T(1024)S(1)}, f32[1024]{0:T(1024)}, u32[]{:S(2)}) copy-start(f32[1024]{0:T(1024)} %param.18) | copy-start | bytes 12292
  83.4 39.4 %all-to-all-start = ((bf16[64,8,1024]{2,1,0:T(8,128)(2,1)}), bf16[64,8,1024]{2,1,0:T(8,128)(2,1)S(1)}, u32[]{:S(2)}, u32[]{:S(2)}) async-start(bf16[64,8,1024]{2,1,0:T(8,128)(2,1)} %scatter_fusion), calls=%async_computation | async-start | bytes 2097152 | tf_op jit(solution)/shard_map/all_to_all | solution.py:69
  94.0 81.2 %all-gather.7.cloned.1.call-start = ((), (), s32[]{:S(2)}) async-start(), calls=%async_computation.4 | async-start | bytes 2359296 | tf_op jit(solution)/shard_map/all_gather | solution.py:83
  128.1 1.4 copy-start.2
  129.4 2.0 copy-start.6
  135.5 124.5 %all-gather.11.cloned.1.call-start = ((), (), s32[]{:S(2)}) async-start(), calls=%async_computation.6 | async-start | bytes 2129920 | tf_op jit(solution)/shard_map/all_gather | solution.py:92
  136.3 207.7 %all-gather.9.cloned.1.call-start = ((), (), s32[]{:S(2)}) async-start(), calls=%async_computation.5 | async-start | bytes 2129920 | tf_op jit(solution)/shard_map/all_gather | solution.py:88
  136.8 207.1 %copy-start.7 = (f32[1024]{0:T(1024)S(1)}, f32[1024]{0:T(1024)}, u32[]{:S(2)}) copy-start(f32[1024]{0:T(1024)} %param.21) | copy-start | bytes 12292
  136.8 263.2 %reduce-scatter.4.cloned.1.call-start = ((), (), s32[]{:S(2)}) async-start(), calls=%async_computation.7 | async-start | bytes 2359296
  175.2 2.2 copy-start.1
Sparse Core Ops, SparseCore 0:
  10.7 88.5 all-gather.4
  135.6 39.5 all-gather.6
  178.6 81.3 all-gather.10
  263.2 80.6 all-gather.8
  356.8 43.1 reduce-scatter.3
where the time goes:
time: 411 us; the launch traced here: 409 us
  waiting for transfers between devices  277 us (67%)
  local copies, waits for them, and re-layouts  67.6 us (16%)
  starting transfers between devices  24.8 us (6%)
  matrix products  18.1 us (4%)
  between operations  13.9 us (3%)
  other arithmetic  8.18 us (2%)
    all_gather x1, waiting for transfers between devices, local(): up_whole = lax.all_gather(up_weight, 'tm', axis=0, tiled=True)  83.9 us
    all_gather x1, waiting for transfers between devices, local(): down_whole = lax.all_gather(down_weight, 'tm', axis=1, tiled=True)  81.9 us
    unnamed x6, waiting for transfers between devices  45.3 us
    all_gather x1, waiting for transfers between devices, local(): window = lax.all_gather(joined, 'grp', axis=0, tiled=True)  38.1 us
    scatter x1, local copies, waits for them, and re-layouts, local(): payload = jnp.zeros((owners, capacity, audio_rows.shape[1]), jnp.bfloat16...  36.2 us
    all_to_all x1, waiting for transfers between devices, local(): lax.all_to_all(payload, 'tm', split_axis=0, concat_axis=0, tiled=True)  27.6 us
    scatter x1, local copies, waits for them, and re-layouts, local(): jnp.full((owners, capacity), -4, jnp.int32).at[destination, slot_index]  21.2 us
    all_to_all x1, starting transfers between devices, local(): lax.all_to_all(band_send, 'tm', split_axis=0, concat_axis=0, tiled=True)  13.8 us
  transfers between devices with their start and end apart: 7, of which 5 were waited for; matrix products, arithmetic and copies ran while one was open for 16% of the time, Pallas kernels for 0%

commit v1 on v0

v1 whole, which is shorter than its diff:
```python
import jax
import jax.numpy as jnp
from jax import lax
from jax.experimental import pallas as pl
from jax.experimental.pallas import tpu as pltpu
from jax.sharding import PartitionSpec as P

HD = 128
BAND_LANES = 128
BAND_SHIFT = 4
WEIGHT_SCALE = 2.0**17
JOINED_SCALE = 0.25


def pack_kernel(owners, capacity, dest_ref, band_ref, rows_ref, out_ref):
    rows = rows_ref.shape[0]
    width = rows_ref.shape[1]
    slots = owners * capacity
    dest = dest_ref[...]
    owner_ids = lax.broadcasted_iota(jnp.int32, (owners, rows), 0)
    named = (owner_ids == dest).astype(jnp.float32)
    before = lax.broadcasted_iota(jnp.int32, (rows, rows), 0) < lax.broadcasted_iota(
        jnp.int32, (rows, rows), 1
    )
    earlier = jnp.dot(
        named.astype(jnp.bfloat16),
        before.astype(jnp.float32).astype(jnp.bfloat16),
        preferred_element_type=jnp.float32,
    )
    slot = jnp.sum(earlier * named, axis=0, keepdims=True).astype(jnp.int32)
    code = dest * capacity + slot
    chosen = lax.broadcasted_iota(jnp.int32, (slots, rows), 0) == code
    chosen_f = chosen.astype(jnp.float32)
    moved = jnp.dot(
        chosen_f.astype(jnp.bfloat16), rows_ref[...], preferred_element_type=jnp.float32
    )
    out_ref[:, :, :width] = moved.astype(jnp.bfloat16).reshape(owners, capacity, width)
    bands = jnp.sum(
        chosen_f * (band_ref[...] + BAND_SHIFT).astype(jnp.float32), axis=1, keepdims=True
    )
    out_ref[:, :, width:] = (
        jnp.broadcast_to(bands, (slots, BAND_LANES))
        .astype(jnp.bfloat16)
        .reshape(owners, capacity, BAND_LANES)
    )


def pack(audio_rows, destination, row_band, owners, capacity):
    rows, width = audio_rows.shape

    def body(*refs):
        pack_kernel(owners, capacity, *refs)

    return pl.pallas_call(
        body,
        out_shape=jax.ShapeDtypeStruct((owners, capacity, width + BAND_LANES), jnp.bfloat16),
        name="pack",
    )(destination.reshape(1, rows), row_band.reshape(1, rows), audio_rows)


def attend_kernel(
    band_ref, slots_ref, latents_ref, query_ref, wk_ref, wv_ref, nk_ref, nv_ref, wo_ref, out_ref, acc_ref
):
    step = pl.program_id(0)
    width = latents_ref.shape[1]
    slots = slots_ref.shape[0] * slots_ref.shape[1]
    scale = 1.0 / float(HD) ** 0.5

    @pl.when(step == 0)
    def _():
        acc_ref[...] = latents_ref[...].astype(jnp.float32)

    frames = slots_ref[:, :, :width].reshape(slots, width)
    bands = slots_ref[:, :, width:].reshape(slots, BAND_LANES).astype(jnp.float32)
    here = (band_ref[0] + BAND_SHIFT).astype(jnp.float32)
    usable = jnp.abs(jnp.transpose(bands) - here) <= 1.0
    keys = jnp.dot(frames, wk_ref[...], preferred_element_type=jnp.float32).astype(jnp.bfloat16)
    values = jnp.dot(frames, wv_ref[...], preferred_element_type=jnp.float32).astype(jnp.bfloat16)
    attended = []
    for h in range(wk_ref.shape[1] // HD):
        cols = slice(h * HD, (h + 1) * HD)
        query = query_ref[:, cols]
        score = (
            lax.dot_general(
                query, keys[:, cols], (((1,), (1,)), ((), ())), preferred_element_type=jnp.float32
            )
            * scale
        )
        null = (
            jnp.sum(query.astype(jnp.float32) * nk_ref[:, cols], axis=1, keepdims=True) * scale
        )
        masked = jnp.where(usable, score, -1e30)
        highest = jnp.maximum(jnp.max(masked, axis=1, keepdims=True), null)
        expo = jnp.where(usable, jnp.exp(masked - highest), 0.0)
        null_expo = jnp.exp(null - highest)
        total = jnp.sum(expo, axis=1, keepdims=True) + null_expo
        inverse = 1.0 / total
        weights = (expo * inverse).astype(jnp.bfloat16)
        null_weight = (null_expo * inverse).astype(jnp.bfloat16).astype(jnp.float32)
        summed = jnp.dot(weights, values[:, cols], preferred_element_type=jnp.float32)
        attended.append((summed + null_weight * nv_ref[:, cols]).astype(jnp.bfloat16))
    acc_ref[...] += jnp.dot(
        jnp.concatenate(attended, axis=1), wo_ref[...], preferred_element_type=jnp.float32
    )

    @pl.when(step == pl.num_programs(0) - 1)
    def _():
        out_ref[...] = acc_ref[...].astype(jnp.bfloat16)


def attend(slots, block_band, latents, wk, wv, null_key, null_value, out_weight):
    count, width = latents.shape
    step = 2 * HD
    return pl.pallas_call(
        attend_kernel,
        grid=(width // step,),
        in_specs=[
            pl.BlockSpec(memory_space=pltpu.SMEM),
            pl.BlockSpec(slots.shape, lambda i: (0, 0, 0)),
            pl.BlockSpec((count, width), lambda i: (0, 0)),
            pl.BlockSpec((count, step), lambda i: (0, i)),
            pl.BlockSpec((width, step), lambda i: (0, i)),
            pl.BlockSpec((width, step), lambda i: (0, i)),
            pl.BlockSpec((1, step), lambda i: (0, i)),
            pl.BlockSpec((1, step), lambda i: (0, i)),
            pl.BlockSpec((step, width), lambda i: (i, 0)),
        ],
        out_specs=pl.BlockSpec((count, width), lambda i: (0, 0)),
        out_shape=jax.ShapeDtypeStruct((count, width), jnp.bfloat16),
        scratch_shapes=[pltpu.VMEM((count, width), jnp.float32)],
        name="attend",
    )(
        block_band,
        slots,
        latents,
        latents,
        wk,
        wv,
        null_key.reshape(1, width),
        null_value.reshape(1, width),
        out_weight,
    )


def local(
    audio_rows,
    routing,
    row_band,
    block_band,
    latents,
    kv_weight,
    null_key,
    null_value,
    out_weight,
    mlp_gain,
    up_weight,
    down_weight,
):
    local_rows = audio_rows.shape[0]
    width = latents.shape[1]
    owners = lax.axis_size("tm")
    groups = lax.axis_size("grp")
    capacity = max(2, 2 * local_rows // owners)

    payload = pack(audio_rows, routing[:, 0], row_band, owners, capacity)
    slots = lax.all_to_all(payload, "tm", split_axis=0, concat_axis=0, tiled=True)

    shard = jnp.concatenate(
        [kv_weight[:, :width], kv_weight[:, width:], up_weight, jnp.transpose(down_weight)], axis=0
    )
    shard = (shard.astype(jnp.float32) * WEIGHT_SCALE).astype(jnp.float16)
    gathered = lax.all_gather(shard, "tm", axis=0, tiled=True)
    gathered = gathered.reshape(owners, 4, kv_weight.shape[0], width)

    def whole(index):
        part = gathered[:, index].astype(jnp.float32) * (1.0 / WEIGHT_SCALE)
        return part.astype(jnp.bfloat16).reshape(width, width)

    joined = attend(
        slots, block_band, latents, whole(0), whole(1), null_key, null_value, out_weight
    )
    sent = (joined.astype(jnp.float32) * JOINED_SCALE).astype(jnp.float16)
    window = lax.all_gather(sent, "grp", axis=0, tiled=True)
    values = window.astype(jnp.float32) * (1.0 / JOINED_SCALE)
    center = values - jnp.mean(values, axis=-1, keepdims=True)
    spread = jnp.mean(center * center, axis=-1, keepdims=True)
    normed = (center * lax.rsqrt(spread + 1e-05) * mlp_gain).astype(jnp.bfloat16)
    hidden = jax.nn.gelu(jnp.dot(normed, whole(2), preferred_element_type=jnp.float32)).astype(
        jnp.bfloat16
    )
    down_rows = whole(3)
    me = lax.axis_index("grp")
    columns = width // groups

    def term(offset):
        owner = lax.rem(me + offset + groups, groups)
        rows = lax.dynamic_slice_in_dim(down_rows, owner * columns, columns, 0)
        return lax.dot_general(
            hidden, rows, (((1,), (1,)), ((), ())), preferred_element_type=jnp.float32
        )

    def hop(values, by):
        pairs = [(i, (i + by) % groups) for i in range(groups)]
        return lax.ppermute(values.astype(jnp.bfloat16), "grp", pairs)

    up_hops = groups // 2
    down_hops = groups - 1 - up_hops
    rising = hop(term(up_hops), 1)
    falling = hop(term(-down_hops), -1)
    for distance in range(1, up_hops):
        rising = hop(rising.astype(jnp.float32) + term(up_hops - distance), 1)
        if distance < down_hops:
            falling = hop(falling.astype(jnp.float32) + term(distance - down_hops), -1)
    residual = lax.dynamic_slice_in_dim(window, me * columns, columns, 1)
    total = term(0) + rising.astype(jnp.float32) + falling.astype(jnp.float32)
    return (residual.astype(jnp.float32) * (1.0 / JOINED_SCALE) + total).astype(jnp.bfloat16)


def solution(mesh):
    return jax.shard_map(
        local,
        mesh=mesh,
        in_specs=(
            P(("grp", "tm"), None),
            P(("grp", "tm"), None),
            P(("grp", "tm")),
            P(("grp", "tm")),
            P(("grp", "tm"), None),
            P("tm", None),
            P(),
            P(),
            P(),
            P(),
            P("tm", "grp"),
            P("grp", "tm"),
        ),
        out_specs=P("tm", "grp"),
        check_vma=False,
    )
```

time: 411 us -> 198 us (0.48)
  the two profiles are of different devices: /device:TPU:4 before, /device:TPU:64 now
where the time goes in v1:
time: 198 us; the launch traced here: 197 us
  blocking collectives  109 us (55%)
  starting transfers between devices  35.5 us (18%)
  waiting for transfers between devices  21 us (11%)
  Pallas kernels  12.6 us (6%)
  matrix products  9.48 us (5%)
  other arithmetic  7.51 us (4%)
    all_gather x1, blocking collectives, local(): gathered = lax.all_gather(shard, 'tm', axis=0, tiled=True)  77.4 us
    all_gather x1, blocking collectives, local(): window = lax.all_gather(sent, 'grp', axis=0, tiled=True)  31.6 us
    ppermute x7, starting transfers between devices, hop(): return lax.ppermute(values.astype(jnp.bfloat16), 'grp', pairs)  22.5 us
    ppermute x7, waiting for transfers between devices, hop(): return lax.ppermute(values.astype(jnp.bfloat16), 'grp', pairs)  21 us
    all_to_all x1, starting transfers between devices, local(): lax.all_to_all(payload, 'tm', split_axis=0, concat_axis=0, tiled=True)  13 us
    pallas_call x1, Pallas kernels, attend(): pl.pallas_call(attend_kernel, grid=(width // step,), in_specs=[pl.BlockSp...  9.79 us
    dot_general x8, matrix products, term(): lax.dot_general(hidden, rows, (((1,), (1,)), ((), ())), preferred_element...  5.77 us
    convert_element_type x1, other arithmetic, whole(): return part.astype(jnp.bfloat16).reshape(width, width)  4.17 us
  transfers between devices with their start and end apart: 8, of which 4 were waited for; matrix products, arithmetic and copies ran while one was open for 4% of the time, Pallas kernels for 0%

profile of v1, /device:TPU:64, one launch (start us, length us, event | category | flops | bytes accessed | tf_op | source)
XLA Modules:
  0.0 197.5 jit_solution(16283126438669961033)
XLA Ops:
  0.0 0.0 copy-start.3
  0.0 0.0 copy-start.4
  0.0 2.8 %pack.1 = bf16[64,8,1152]{2,1,0:T(8,128)(2,1)} custom-call(s32[1,256]{1,0:T(1,128)} %bitcast.50, s32[1,256]{1,0:T(1,128)} %bitcast.51, bf16[256,1024]{1,0:T(8,128)(2,1)} %refs_2_.1), custom_call_target="tpu_custom_call" | custom-call | tf_op jit(solution)/shard_map/pack/pallas_call | solution.py:54
  2.8 13.0 %all-to-all-start = ((bf16[64,8,1152]{2,1,0:T(8,128)(2,1)}), bf16[64,8,1152]{2,1,0:T(8,128)(2,1)S(1)}, u32[]{:S(2)}, u32[]{:S(2)}) async-start(bf16[64,8,1152]{2,1,0:T(8,128)(2,1)} %pack.1), calls=%async_computation | async-start | bytes 2359296 | tf_op jit(solution)/shard_map/all_to_all | solution.py:166
  15.8 0.0 copy-done.2
  16.5 0.0 copy-done.3
  16.6 0.0 copy-done.4
  16.6 77.4 %all-gather.2 = f16[4096,1024]{1,0:T(8,128)(2,1)S(1)} all-gather(f16[64,1024]{1,0:T(8,128)(2,1)S(1)} %multiply_convert_fusion.9), channel_id=1, replica_groups=mesh['grp'=8,'tm'=64] {'tm'}, dimensions={0}, use_global_device_ids=true | all-gather | bytes 8519680 | tf_op jit(solution)/shard_map/all_gather | solution.py:172
  94.0 4.2 %multiply_convert_fusion = (bf16[64,1,16,1024]{3,2,0,1:T(8,128)(2,1)S(1)}, bf16[64,1,16,1024]{3,2,0,1:T(8,128)(2,1)}, bf16[64,1,16,1024]{3,2,0,1:T(8,128)(2,1)}, bf16[64,1,16,1024]{3,2,0,1:T(8,128)(2,1)}) fusion(f16[64,4,16,1024]{3,2,1,0:T(8,128)(2,1)S(1)} %bitcast.35), kind=kLoop, calls=%fused_computation.9 | loop fusion | flops 12582912 | bytes 16777216 | tf_op jit(solution)/shard_map/convert_element_type | solution.py:177
  98.2 0.0 all-to-all-done.slots_ref
  98.2 0.0 copy-start
  98.2 1.0 copy-done
  99.2 9.8 %attend.1 = bf16[128,1024]{1,0:T(8,128)(2,1)} custom-call(s32[1]{0:T(128)S(6)} %copy.21.band_ref, bf16[64,8,1152]{2,1,0:T(8,128)(2,1)} %copy-done, bf16[128,1024]{1,0:T(8,128)(2,1)} %query_ref.1, bf16[128,1024]{1,0:T(8,128)(2,1)} %query_ref.1, bf16[1024,1024]{1,0:T(8,128)(2,1)} %bitcast.37, bf16[1024,1024]{1,0:T(8,128)(2,1)} %bitcast.36, ...), custom_call_target="tpu_custom_call" | custom-call | tf_op jit(solution)/shard_map/attend/pallas_call | solution.py:114
  109.0 1.0 multiply_convert_fusion.8
  110.1 31.6 %all-gather.3 = f16[1024,1024]{1,0:T(8,128)(2,1)S(1)} all-gather(f16[128,1024]{1,0:T(8,128)(2,1)S(1)} %multiply_convert_fusion.8), channel_id=1, replica_groups=mesh['grp'=8,'tm'=64] {'grp'}, dimensions={0}, use_global_device_ids=true | all-gather | bytes 2359296 | tf_op jit(solution)/shard_map/all_gather | solution.py:183
  141.7 0.0 copy-start.1
  141.7 0.0 copy-start.5
  141.7 0.5 fusion.9
  142.2 0.8 multiply_reduce_fusion
  143.0 0.3 copy-done.1
  143.3 0.0 copy-done.5
  143.3 3.7 %fusion.7 = bf16[1024,1024]{1,0:T(8,128)(2,1)S(1)} fusion(bf16[1024,1024]{1,0:T(8,128)(2,1)S(1)} %bitcast.46, f16[1024,1024]{1,0:T(8,128)(2,1)S(1)} %all-gather.3, f32[1024]{0:T(1024)S(1)} %copy-done.5, f32[1024]{0:T(1024)S(1)} %add_rsqrt_fusion, f32[1024]{0:T(1024)S(1)} %broadcast_multiply_fusion), kind=kOutput, calls=%fused_computation.8 | convolution fusion | flops 2163212288 | bytes 6303744 | tf_op jit(solution)/shard_map/dot_general | solution.py:188
  147.0 0.7 fusion.15
  147.7 0.7 convolution_convert_fusion
  148.5 4.2 %collective-permute-start.4 = (bf16[1024,128]{1,0:T(8,128)(2,1)S(1)}, bf16[1024,128]{1,0:T(8,128)(2,1)S(1)}, u32[]{:S(2)}, u32[]{:S(2)}) collective-permute-start(bf16[1024,128]{1,0:T(8,128)(2,1)S(1)} %convolution_convert_fusion), channel_id=1, source_target_pairs={{0,448},{64,0},{128,64},{192,128},{256,192},{320,256},{384,320},{4... | collective-permute-start | bytes 786440 | tf_op jit(solution)/shard_map/ppermute | solution.py:204
  152.7 0.7 convolution_convert_fusion.1
  153.4 2.1 %collective-permute-start = (bf16[1024,128]{1,0:T(8,128)(2,1)S(1)}, bf16[1024,128]{1,0:T(8,128)(2,1)S(1)}, u32[]{:S(2)}, u32[]{:S(2)}) collective-permute-start(bf16[1024,128]{1,0:T(8,128)(2,1)S(1)} %convolution_convert_fusion.1), channel_id=1, source_target_pairs={{0,64},{64,128},{128,192},{192,256},{256,320},{320,384},{384,448},... | collective-permute-start | bytes 786440 | tf_op jit(solution)/shard_map/ppermute | solution.py:204
  155.5 0.7 fusion.24
  156.2 6.6 %collective-permute-done = bf16[1024,128]{1,0:T(8,128)(2,1)S(1)} collective-permute-done((bf16[1024,128]{1,0:T(8,128)(2,1)S(1)}, bf16[1024,128]{1,0:T(8,128)(2,1)S(1)}, u32[]{:S(2)}, u32[]{:S(2)}) %collective-permute-start) | collective-permute-done | bytes 262176 | tf_op jit(solution)/shard_map/ppermute | solution.py:204
  162.9 0.7 add_convert_fusion.5
  163.6 1.9 collective-permute-start.1
  165.5 0.0 collective-permute-done.4
  165.5 0.7 add_convert_fusion.2
  166.3 5.1 %collective-permute-start.5 = (bf16[1024,128]{1,0:T(8,128)(2,1)S(1)}, bf16[1024,128]{1,0:T(8,128)(2,1)S(1)}, u32[]{:S(2)}, u32[]{:S(2)}) collective-permute-start(bf16[1024,128]{1,0:T(8,128)(2,1)S(1)} %add_convert_fusion.2), channel_id=1, source_target_pairs={{0,448},{64,0},{128,64},{192,128},{256,192},{320,256},{384,320},{4... | collective-permute-start | bytes 786440 | tf_op jit(solution)/shard_map/ppermute | solution.py:204
  171.4 3.4 %collective-permute-done.1 = bf16[1024,128]{1,0:T(8,128)(2,1)S(1)} collective-permute-done((bf16[1024,128]{1,0:T(8,128)(2,1)S(1)}, bf16[1024,128]{1,0:T(8,128)(2,1)S(1)}, u32[]{:S(2)}, u32[]{:S(2)}) %collective-permute-start.1) | collective-permute-done | bytes 262176 | tf_op jit(solution)/shard_map/ppermute | solution.py:204
  174.8 0.1 add_convert_fusion.4
  174.9 1.9 collective-permute-start.2
  176.8 0.7 fusion.22
  177.5 0.0 collective-permute-done.5
  177.6 0.1 add_convert_fusion.1
  177.6 5.3 %collective-permute-start.6 = (bf16[1024,128]{1,0:T(8,128)(2,1)S(1)}, bf16[1024,128]{1,0:T(8,128)(2,1)S(1)}, u32[]{:S(2)}, u32[]{:S(2)}) collective-permute-start(bf16[1024,128]{1,0:T(8,128)(2,1)S(1)} %add_convert_fusion.1), channel_id=1, source_target_pairs={{0,448},{64,0},{128,64},{192,128},{256,192},{320,256},{384,320},{4... | collective-permute-start | bytes 786440 | tf_op jit(solution)/shard_map/ppermute | solution.py:204
  183.0 4.1 %collective-permute-done.2 = bf16[1024,128]{1,0:T(8,128)(2,1)S(1)} collective-permute-done((bf16[1024,128]{1,0:T(8,128)(2,1)S(1)}, bf16[1024,128]{1,0:T(8,128)(2,1)S(1)}, u32[]{:S(2)}, u32[]{:S(2)}) %collective-permute-start.2) | collective-permute-done | bytes 262176 | tf_op jit(solution)/shard_map/ppermute | solution.py:204
  187.1 0.1 add_convert_fusion.3
  187.1 1.9 collective-permute-start.3
  189.1 0.7 fusion.31
  189.8 0.0 collective-permute-done.6
  189.8 6.8 %collective-permute-done.3 = bf16[1024,128]{1,0:T(8,128)(2,1)S(1)} collective-permute-done((bf16[1024,128]{1,0:T(8,128)(2,1)S(1)}, bf16[1024,128]{1,0:T(8,128)(2,1)S(1)}, u32[]{:S(2)}, u32[]{:S(2)}) %collective-permute-start.3) | collective-permute-done | bytes 262176 | tf_op jit(solution)/shard_map/ppermute | solution.py:204
  196.6 0.9 add_convert_fusion
  (5 shorter events, 0.1 us)
Async XLA Ops:
  0.0 15.8 %copy-start.2 = (bf16[16,2048]{1,0:T(8,128)(2,1)S(1)}, bf16[16,2048]{1,0:T(8,128)(2,1)}, u32[]{:S(2)}) copy-start(bf16[16,2048]{1,0:T(8,128)(2,1)} %param.17) | copy-start | bytes 196612
  0.0 16.5 %copy-start.3 = (bf16[1024,16]{0,1:T(8,128)(2,1)S(1)}, bf16[1024,16]{0,1:T(8,128)(2,1)}, u32[]{:S(2)}) copy-start(bf16[1024,16]{0,1:T(8,128)(2,1)} %param.23) | copy-start | bytes 98308
  0.0 16.6 %copy-start.4 = (bf16[16,1024]{1,0:T(8,128)(2,1)S(1)}, bf16[16,1024]{1,0:T(8,128)(2,1)}, u32[]{:S(2)}) copy-start(bf16[16,1024]{1,0:T(8,128)(2,1)} %param.22) | copy-start | bytes 98308
  2.8 95.4 %all-to-all-start = ((bf16[64,8,1152]{2,1,0:T(8,128)(2,1)}), bf16[64,8,1152]{2,1,0:T(8,128)(2,1)S(1)}, u32[]{:S(2)}, u32[]{:S(2)}) async-start(bf16[64,8,1152]{2,1,0:T(8,128)(2,1)} %pack.1), calls=%async_computation | async-start | bytes 2359296 | tf_op jit(solution)/shard_map/all_to_all | solution.py:166
  98.2 1.0 copy-start
  141.7 1.6 copy-start.1
  141.7 1.6 copy-start.5
  148.5 17.1 %collective-permute-start.4 = (bf16[1024,128]{1,0:T(8,128)(2,1)S(1)}, bf16[1024,128]{1,0:T(8,128)(2,1)S(1)}, u32[]{:S(2)}, u32[]{:S(2)}) collective-permute-start(bf16[1024,128]{1,0:T(8,128)(2,1)S(1)} %convolution_convert_fusion), channel_id=1, source_target_pairs={{0,448},{64,0},{128,64},{192,128},{256,192},{320,256},{384,320},{4... | collective-permute-start | bytes 786440 | tf_op jit(solution)/shard_map/ppermute | solution.py:204
  153.4 9.5 %collective-permute-start = (bf16[1024,128]{1,0:T(8,128)(2,1)S(1)}, bf16[1024,128]{1,0:T(8,128)(2,1)S(1)}, u32[]{:S(2)}, u32[]{:S(2)}) collective-permute-start(bf16[1024,128]{1,0:T(8,128)(2,1)S(1)} %convolution_convert_fusion.1), channel_id=1, source_target_pairs={{0,64},{64,128},{128,192},{192,256},{256,320},{320,384},{384,448},... | collective-permute-start | bytes 786440 | tf_op jit(solution)/shard_map/ppermute | solution.py:204
  163.6 11.2 %collective-permute-start.1 = (bf16[1024,128]{1,0:T(8,128)(2,1)S(1)}, bf16[1024,128]{1,0:T(8,128)(2,1)S(1)}, u32[]{:S(2)}, u32[]{:S(2)}) collective-permute-start(bf16[1024,128]{1,0:T(8,128)(2,1)S(1)} %add_convert_fusion.5), channel_id=1, source_target_pairs={{0,64},{64,128},{128,192},{192,256},{256,320},{320,384},{384,448},... | collective-permute-start | bytes 786440 | tf_op jit(solution)/shard_map/ppermute | solution.py:204
  166.3 11.3 %collective-permute-start.5 = (bf16[1024,128]{1,0:T(8,128)(2,1)S(1)}, bf16[1024,128]{1,0:T(8,128)(2,1)S(1)}, u32[]{:S(2)}, u32[]{:S(2)}) collective-permute-start(bf16[1024,128]{1,0:T(8,128)(2,1)S(1)} %add_convert_fusion.2), channel_id=1, source_target_pairs={{0,448},{64,0},{128,64},{192,128},{256,192},{320,256},{384,320},{4... | collective-permute-start | bytes 786440 | tf_op jit(solution)/shard_map/ppermute | solution.py:204
  174.9 12.2 %collective-permute-start.2 = (bf16[1024,128]{1,0:T(8,128)(2,1)S(1)}, bf16[1024,128]{1,0:T(8,128)(2,1)S(1)}, u32[]{:S(2)}, u32[]{:S(2)}) collective-permute-start(bf16[1024,128]{1,0:T(8,128)(2,1)S(1)} %add_convert_fusion.4), channel_id=1, source_target_pairs={{0,64},{64,128},{128,192},{192,256},{256,320},{320,384},{384,448},... | collective-permute-start | bytes 786440 | tf_op jit(solution)/shard_map/ppermute | solution.py:204
  177.6 12.2 %collective-permute-start.6 = (bf16[1024,128]{1,0:T(8,128)(2,1)S(1)}, bf16[1024,128]{1,0:T(8,128)(2,1)S(1)}, u32[]{:S(2)}, u32[]{:S(2)}) collective-permute-start(bf16[1024,128]{1,0:T(8,128)(2,1)S(1)} %add_convert_fusion.1), channel_id=1, source_target_pairs={{0,448},{64,0},{128,64},{192,128},{256,192},{320,256},{384,320},{4... | collective-permute-start | bytes 786440 | tf_op jit(solution)/shard_map/ppermute | solution.py:204
  187.1 9.5 %collective-permute-start.3 = (bf16[1024,128]{1,0:T(8,128)(2,1)S(1)}, bf16[1024,128]{1,0:T(8,128)(2,1)S(1)}, u32[]{:S(2)}, u32[]{:S(2)}) collective-permute-start(bf16[1024,128]{1,0:T(8,128)(2,1)S(1)} %add_convert_fusion.3), channel_id=1, source_target_pairs={{0,64},{64,128},{128,192},{192,256},{256,320},{320,384},{384,448},... | collective-permute-start | bytes 786440 | tf_op jit(solution)/shard_map/ppermute | solution.py:204

commit v2 on v1

--- a/solution.py
+++ b/solution.py
@@ -4,6 +4,7 @@
 from jax.experimental import pallas as pl
 from jax.experimental.pallas import tpu as pltpu
 from jax.sharding import PartitionSpec as P
+
 
 HD = 128
 BAND_LANES = 128
@@ -59,7 +60,18 @@
 
 
 def attend_kernel(
-    band_ref, slots_ref, latents_ref, query_ref, wk_ref, wv_ref, nk_ref, nv_ref, wo_ref, out_ref, acc_ref
+    band_ref,
+    slots_ref,
+    latents_ref,
+    query_ref,
+    wk_ref,
+    wv_ref,
+    nk_ref,
+    nv_ref,
+    wo_ref,
+    out_ref,
+    acc_ref,
+    away_ref,
 ):
     step = pl.program_id(0)
     width = latents_ref.shape[1]
@@ -69,11 +81,12 @@
     @pl.when(step == 0)
     def _():
         acc_ref[...] = latents_ref[...].astype(jnp.float32)
+        bands = slots_ref[:, :, width:].reshape(slots, BAND_LANES).astype(jnp.float32)
+        here = (band_ref[0] + BAND_SHIFT).astype(jnp.float32)
+        away_ref[...] = jnp.abs(jnp.transpose(bands) - here)
 
     frames = slots_ref[:, :, :width].reshape(slots, width)
-    bands = slots_ref[:, :, width:].reshape(slots, BAND_LANES).astype(jnp.float32)
-    here = (band_ref[0] + BAND_SHIFT).astype(jnp.float32)
-    usable = jnp.abs(jnp.transpose(bands) - here) <= 1.0
+    usable = away_ref[...] <= 1.0
     keys = jnp.dot(frames, wk_ref[...], preferred_element_type=jnp.float32).astype(jnp.bfloat16)
     values = jnp.dot(frames, wv_ref[...], preferred_element_type=jnp.float32).astype(jnp.bfloat16)
     attended = []
@@ -110,7 +123,7 @@
 
 def attend(slots, block_band, latents, wk, wv, null_key, null_value, out_weight):
     count, width = latents.shape
-    step = 2 * HD
+    step = 4 * HD
     return pl.pallas_call(
         attend_kernel,
         grid=(width // step,),
@@ -127,7 +140,10 @@
         ],
         out_specs=pl.BlockSpec((count, width), lambda i: (0, 0)),
         out_shape=jax.ShapeDtypeStruct((count, width), jnp.bfloat16),
-        scratch_shapes=[pltpu.VMEM((count, width), jnp.float32)],
+        scratch_shapes=[
+            pltpu.VMEM((count, width), jnp.float32),
+            pltpu.VMEM((count, slots.shape[0] * slots.shape[1]), jnp.float32),
+        ],
         name="attend",
     )(
         block_band,
@@ -195,13 +211,16 @@
     def term(offset):
         owner = lax.rem(me + offset + groups, groups)
         rows = lax.dynamic_slice_in_dim(down_rows, owner * columns, columns, 0)
-        return lax.dot_general(
-            hidden, rows, (((1,), (1,)), ((), ())), preferred_element_type=jnp.float32
+        return lax.optimization_barrier(
+            lax.dot_general(
+                hidden, rows, (((1,), (1,)), ((), ())), preferred_element_type=jnp.float32
+            )
         )
 
     def hop(values, by):
         pairs = [(i, (i + by) % groups) for i in range(groups)]
-        return lax.ppermute(values.astype(jnp.bfloat16), "grp", pairs)
+        values = values.astype(jnp.bfloat16)
+        return lax.ppermute(values, "grp", pairs)
 
     up_hops = groups // 2
     down_hops = groups - 1 - up_hops

time: 198 us -> 198 us (level)
  no operation moved by 1% of the time
where the time goes in v2:
time: 198 us
  blocking collectives  109 us (55%)
  starting transfers between devices  35.6 us (18%)
  waiting for transfers between devices  21.7 us (11%)
  Pallas kernels  12.1 us (6%)
  matrix products  9.45 us (5%)
  other arithmetic  7.62 us (4%)
    all_gather x1, blocking collectives, local(): gathered = lax.all_gather(shard, 'tm', axis=0, tiled=True)  77.4 us
    all_gather x1, blocking collectives, local(): window = lax.all_gather(sent, 'grp', axis=0, tiled=True)  31.7 us
    ppermute x7, starting transfers between devices, hop(): return lax.ppermute(values, 'grp', pairs)  22.6 us
    ppermute x7, waiting for transfers between devices, hop(): return lax.ppermute(values, 'grp', pairs)  21.7 us
    all_to_all x1, starting transfers between devices, local(): lax.all_to_all(payload, 'tm', split_axis=0, concat_axis=0, tiled=True)  13 us
    pallas_call x1, Pallas kernels, attend(): pl.pallas_call(attend_kernel, grid=(width // step,), in_specs=[pl.BlockSp...  9.35 us
    dot_general x8, matrix products, term(): lax.dot_general(hidden, rows, (((1,), (1,)), ((), ())), preferred_element...  5.74 us
    convert_element_type x1, other arithmetic, whole(): return part.astype(jnp.bfloat16).reshape(width, width)  4.17 us
  transfers between devices with their start and end apart: 8, of which 4 were waited for; matrix products, arithmetic and copies ran while one was open for 4% of the time, Pallas kernels for 0%

profile of v2, /device:TPU:64, one launch (start us, length us, event | category | flops | bytes accessed | tf_op | source)
XLA Modules:
  0.0 197.9 jit_solution(15797533106839776180)
XLA Ops:
  0.0 0.0 copy-start.2
  0.0 0.0 copy-start.3
  0.0 0.0 copy-start.4
  0.0 2.8 %pack.1 = bf16[64,8,1152]{2,1,0:T(8,128)(2,1)} custom-call(s32[1,256]{1,0:T(1,128)} %bitcast.50, s32[1,256]{1,0:T(1,128)} %bitcast.51, bf16[256,1024]{1,0:T(8,128)(2,1)} %refs_2_.1), custom_call_target="tpu_custom_call" | custom-call | tf_op jit(solution)/shard_map/pack/pallas_call | solution.py:55
  2.8 13.0 %all-to-all-start = ((bf16[64,8,1152]{2,1,0:T(8,128)(2,1)}), bf16[64,8,1152]{2,1,0:T(8,128)(2,1)S(1)}, u32[]{:S(2)}, u32[]{:S(2)}) async-start(bf16[64,8,1152]{2,1,0:T(8,128)(2,1)} %pack.1), calls=%async_computation | async-start | bytes 2359296 | tf_op jit(solution)/shard_map/all_to_all | solution.py:182
  15.8 0.0 copy-done.2
  16.5 0.0 copy-done.3
  16.6 0.0 copy-done.4
  16.6 77.4 %all-gather.2 = f16[4096,1024]{1,0:T(8,128)(2,1)S(1)} all-gather(f16[64,1024]{1,0:T(8,128)(2,1)S(1)} %multiply_convert_fusion.9), channel_id=1, replica_groups=mesh['grp'=8,'tm'=64] {'tm'}, dimensions={0}, use_global_device_ids=true | all-gather | bytes 8519680 | tf_op jit(solution)/shard_map/all_gather | solution.py:188
  94.0 4.2 %multiply_convert_fusion = (bf16[64,1,16,1024]{3,2,0,1:T(8,128)(2,1)S(1)}, bf16[64,1,16,1024]{3,2,0,1:T(8,128)(2,1)}, bf16[64,1,16,1024]{3,2,0,1:T(8,128)(2,1)}, bf16[64,1,16,1024]{3,2,0,1:T(8,128)(2,1)}) fusion(f16[64,4,16,1024]{3,2,1,0:T(8,128)(2,1)S(1)} %bitcast.35), kind=kLoop, calls=%fused_computation.9 | loop fusion | flops 12582912 | bytes 16777216 | tf_op jit(solution)/shard_map/convert_element_type | solution.py:193
  98.2 0.0 all-to-all-done.slots_ref
  98.2 1.0 copy-done
  99.2 9.4 %attend.1 = bf16[128,1024]{1,0:T(8,128)(2,1)} custom-call(s32[1]{0:T(128)S(6)} %copy.21.band_ref, bf16[64,8,1152]{2,1,0:T(8,128)(2,1)} %copy-done, bf16[128,1024]{1,0:T(8,128)(2,1)} %query_ref.1, bf16[128,1024]{1,0:T(8,128)(2,1)} %query_ref.1, bf16[1024,1024]{1,0:T(8,128)(2,1)} %bitcast.37, bf16[1024,1024]{1,0:T(8,128)(2,1)} %bitcast.36, ...), custom_call_target="tpu_custom_call" | custom-call | tf_op jit(solution)/shard_map/attend/pallas_call | solution.py:127
  108.6 1.0 multiply_convert_fusion.8
  109.6 31.7 %all-gather.3 = f16[1024,1024]{1,0:T(8,128)(2,1)S(1)} all-gather(f16[128,1024]{1,0:T(8,128)(2,1)S(1)} %multiply_convert_fusion.8), channel_id=1, replica_groups=mesh['grp'=8,'tm'=64] {'grp'}, dimensions={0}, use_global_device_ids=true | all-gather | bytes 2359296 | tf_op jit(solution)/shard_map/all_gather | solution.py:199
  141.3 0.5 fusion.9
  141.8 0.8 multiply_reduce_fusion
  142.6 0.3 copy-done.1
  142.9 0.0 copy-done.5
  142.9 3.7 %fusion.7 = bf16[1024,1024]{1,0:T(8,128)(2,1)S(1)} fusion(bf16[1024,1024]{1,0:T(8,128)(2,1)S(1)} %bitcast.46, f16[1024,1024]{1,0:T(8,128)(2,1)S(1)} %all-gather.3, f32[1024]{0:T(1024)S(1)} %copy-done.5, f32[1024]{0:T(1024)S(1)} %add_rsqrt_fusion, f32[1024]{0:T(1024)S(1)} %broadcast_multiply_fusion), kind=kOutput, calls=%fused_computation.8 | convolution fusion | flops 2163212288 | bytes 6303744 | tf_op jit(solution)/shard_map/dot_general | solution.py:204
  146.6 0.7 fusion.15
  147.3 0.7 fusion.19
  148.0 4.4 %collective-permute-start.4 = (bf16[1024,128]{1,0:T(8,128)(2,1)S(1)}, bf16[1024,128]{1,0:T(8,128)(2,1)S(1)}, u32[]{:S(2)}, u32[]{:S(2)}) collective-permute-start(bf16[1024,128]{1,0:T(8,128)(2,1)S(1)} %fusion.19), channel_id=1, source_target_pairs={{0,448},{64,0},{128,64},{192,128},{256,192},{320,256},{384,320},{4... | collective-permute-start | bytes 786440 | tf_op jit(solution)/shard_map/ppermute | solution.py:223
  152.4 0.7 fusion.25
  153.1 0.7 fusion.27
  153.9 1.9 collective-permute-start
  155.8 0.7 fusion.17
  156.5 7.4 %collective-permute-done = bf16[1024,128]{1,0:T(8,128)(2,1)S(1)} collective-permute-done((bf16[1024,128]{1,0:T(8,128)(2,1)S(1)}, bf16[1024,128]{1,0:T(8,128)(2,1)S(1)}, u32[]{:S(2)}, u32[]{:S(2)}) %collective-permute-start) | collective-permute-done | bytes 262176 | tf_op jit(solution)/shard_map/ppermute | solution.py:223
  163.9 0.1 add_convert_fusion.5
  164.0 1.9 collective-permute-start.1
  165.9 0.7 fusion.23
  166.7 0.0 collective-permute-done.4
  166.7 0.1 add_convert_fusion.2
  166.7 5.1 %collective-permute-start.5 = (bf16[1024,128]{1,0:T(8,128)(2,1)S(1)}, bf16[1024,128]{1,0:T(8,128)(2,1)S(1)}, u32[]{:S(2)}, u32[]{:S(2)}) collective-permute-start(bf16[1024,128]{1,0:T(8,128)(2,1)S(1)} %add_convert_fusion.2), channel_id=1, source_target_pairs={{0,448},{64,0},{128,64},{192,128},{256,192},{320,256},{384,320},{4... | collective-permute-start | bytes 786440 | tf_op jit(solution)/shard_map/ppermute | solution.py:223
  171.9 3.4 %collective-permute-done.1 = bf16[1024,128]{1,0:T(8,128)(2,1)S(1)} collective-permute-done((bf16[1024,128]{1,0:T(8,128)(2,1)S(1)}, bf16[1024,128]{1,0:T(8,128)(2,1)S(1)}, u32[]{:S(2)}, u32[]{:S(2)}) %collective-permute-start.1) | collective-permute-done | bytes 262176 | tf_op jit(solution)/shard_map/ppermute | solution.py:223
  175.2 0.1 add_convert_fusion.4
  175.3 1.9 collective-permute-start.2
  177.2 0.7 fusion.21
  177.9 0.0 collective-permute-done.5
  178.0 0.1 add_convert_fusion.1
  178.0 5.4 %collective-permute-start.6 = (bf16[1024,128]{1,0:T(8,128)(2,1)S(1)}, bf16[1024,128]{1,0:T(8,128)(2,1)S(1)}, u32[]{:S(2)}, u32[]{:S(2)}) collective-permute-start(bf16[1024,128]{1,0:T(8,128)(2,1)S(1)} %add_convert_fusion.1), channel_id=1, source_target_pairs={{0,448},{64,0},{128,64},{192,128},{256,192},{320,256},{384,320},{4... | collective-permute-start | bytes 786440 | tf_op jit(solution)/shard_map/ppermute | solution.py:223
  183.4 4.0 %collective-permute-done.2 = bf16[1024,128]{1,0:T(8,128)(2,1)S(1)} collective-permute-done((bf16[1024,128]{1,0:T(8,128)(2,1)S(1)}, bf16[1024,128]{1,0:T(8,128)(2,1)S(1)}, u32[]{:S(2)}, u32[]{:S(2)}) %collective-permute-start.2) | collective-permute-done | bytes 262176 | tf_op jit(solution)/shard_map/ppermute | solution.py:223
  187.5 0.1 add_convert_fusion.3
  187.5 1.9 collective-permute-start.3
  189.5 0.7 fusion.29
  190.2 0.0 collective-permute-done.6
  190.2 6.8 %collective-permute-done.3 = bf16[1024,128]{1,0:T(8,128)(2,1)S(1)} collective-permute-done((bf16[1024,128]{1,0:T(8,128)(2,1)S(1)}, bf16[1024,128]{1,0:T(8,128)(2,1)S(1)}, u32[]{:S(2)}, u32[]{:S(2)}) %collective-permute-start.3) | collective-permute-done | bytes 262176 | tf_op jit(solution)/shard_map/ppermute | solution.py:223
  197.0 0.9 add_convert_fusion
  (7 shorter events, 0.1 us)
Async XLA Ops:
  0.0 15.8 %copy-start.2 = (bf16[16,2048]{1,0:T(8,128)(2,1)S(1)}, bf16[16,2048]{1,0:T(8,128)(2,1)}, u32[]{:S(2)}) copy-start(bf16[16,2048]{1,0:T(8,128)(2,1)} %param.17) | copy-start | bytes 196612
  0.0 16.5 %copy-start.3 = (bf16[1024,16]{0,1:T(8,128)(2,1)S(1)}, bf16[1024,16]{0,1:T(8,128)(2,1)}, u32[]{:S(2)}) copy-start(bf16[1024,16]{0,1:T(8,128)(2,1)} %param.23) | copy-start | bytes 98308
  0.0 16.6 %copy-start.4 = (bf16[16,1024]{1,0:T(8,128)(2,1)S(1)}, bf16[16,1024]{1,0:T(8,128)(2,1)}, u32[]{:S(2)}) copy-start(bf16[16,1024]{1,0:T(8,128)(2,1)} %param.22) | copy-start | bytes 98308
  2.8 95.4 %all-to-all-start = ((bf16[64,8,1152]{2,1,0:T(8,128)(2,1)}), bf16[64,8,1152]{2,1,0:T(8,128)(2,1)S(1)}, u32[]{:S(2)}, u32[]{:S(2)}) async-start(bf16[64,8,1152]{2,1,0:T(8,128)(2,1)} %pack.1), calls=%async_computation | async-start | bytes 2359296 | tf_op jit(solution)/shard_map/all_to_all | solution.py:182
  98.2 1.0 copy-start
  141.3 1.6 copy-start.1
  141.3 1.6 copy-start.5
  148.0 18.6 %collective-permute-start.4 = (bf16[1024,128]{1,0:T(8,128)(2,1)S(1)}, bf16[1024,128]{1,0:T(8,128)(2,1)S(1)}, u32[]{:S(2)}, u32[]{:S(2)}) collective-permute-start(bf16[1024,128]{1,0:T(8,128)(2,1)S(1)} %fusion.19), channel_id=1, source_target_pairs={{0,448},{64,0},{128,64},{192,128},{256,192},{320,256},{384,320},{4... | collective-permute-start | bytes 786440 | tf_op jit(solution)/shard_map/ppermute | solution.py:223
  153.9 10.1 %collective-permute-start = (bf16[1024,128]{1,0:T(8,128)(2,1)S(1)}, bf16[1024,128]{1,0:T(8,128)(2,1)S(1)}, u32[]{:S(2)}, u32[]{:S(2)}) collective-permute-start(bf16[1024,128]{1,0:T(8,128)(2,1)S(1)} %fusion.27), channel_id=1, source_target_pairs={{0,64},{64,128},{128,192},{192,256},{256,320},{320,384},{384,448},... | collective-permute-start | bytes 786440 | tf_op jit(solution)/shard_map/ppermute | solution.py:223
  164.0 11.2 %collective-permute-start.1 = (bf16[1024,128]{1,0:T(8,128)(2,1)S(1)}, bf16[1024,128]{1,0:T(8,128)(2,1)S(1)}, u32[]{:S(2)}, u32[]{:S(2)}) collective-permute-start(bf16[1024,128]{1,0:T(8,128)(2,1)S(1)} %add_convert_fusion.5), channel_id=1, source_target_pairs={{0,64},{64,128},{128,192},{192,256},{256,320},{320,384},{384,448},... | collective-permute-start | bytes 786440 | tf_op jit(solution)/shard_map/ppermute | solution.py:223
  166.7 11.2 %collective-permute-start.5 = (bf16[1024,128]{1,0:T(8,128)(2,1)S(1)}, bf16[1024,128]{1,0:T(8,128)(2,1)S(1)}, u32[]{:S(2)}, u32[]{:S(2)}) collective-permute-start(bf16[1024,128]{1,0:T(8,128)(2,1)S(1)} %add_convert_fusion.2), channel_id=1, source_target_pairs={{0,448},{64,0},{128,64},{192,128},{256,192},{320,256},{384,320},{4... | collective-permute-start | bytes 786440 | tf_op jit(solution)/shard_map/ppermute | solution.py:223
  175.3 12.2 %collective-permute-start.2 = (bf16[1024,128]{1,0:T(8,128)(2,1)S(1)}, bf16[1024,128]{1,0:T(8,128)(2,1)S(1)}, u32[]{:S(2)}, u32[]{:S(2)}) collective-permute-start(bf16[1024,128]{1,0:T(8,128)(2,1)S(1)} %add_convert_fusion.4), channel_id=1, source_target_pairs={{0,64},{64,128},{128,192},{192,256},{256,320},{320,384},{384,448},... | collective-permute-start | bytes 786440 | tf_op jit(solution)/shard_map/ppermute | solution.py:223
  178.0 12.2 %collective-permute-start.6 = (bf16[1024,128]{1,0:T(8,128)(2,1)S(1)}, bf16[1024,128]{1,0:T(8,128)(2,1)S(1)}, u32[]{:S(2)}, u32[]{:S(2)}) collective-permute-start(bf16[1024,128]{1,0:T(8,128)(2,1)S(1)} %add_convert_fusion.1), channel_id=1, source_target_pairs={{0,448},{64,0},{128,64},{192,128},{256,192},{320,256},{384,320},{4... | collective-permute-start | bytes 786440 | tf_op jit(solution)/shard_map/ppermute | solution.py:223
  187.5 9.5 %collective-permute-start.3 = (bf16[1024,128]{1,0:T(8,128)(2,1)S(1)}, bf16[1024,128]{1,0:T(8,128)(2,1)S(1)}, u32[]{:S(2)}, u32[]{:S(2)}) collective-permute-start(bf16[1024,128]{1,0:T(8,128)(2,1)S(1)} %add_convert_fusion.3), channel_id=1, source_target_pairs={{0,64},{64,128},{128,192},{192,256},{256,320},{320,384},{384,448},... | collective-permute-start | bytes 786440 | tf_op jit(solution)/shard_map/ppermute | solution.py:223

commit v3 on v2

--- a/solution.py
+++ b/solution.py
@@ -8,6 +8,8 @@
 
 HD = 128
 BAND_LANES = 128
+FEATURES = 128
+LINES = 8
 BAND_SHIFT = 4
 WEIGHT_SCALE = 2.0**17
 JOINED_SCALE = 0.25
@@ -72,6 +74,7 @@
     out_ref,
     acc_ref,
     away_ref,
+    frames_ref,
 ):
     step = pl.program_id(0)
     width = latents_ref.shape[1]
@@ -84,8 +87,15 @@
         bands = slots_ref[:, :, width:].reshape(slots, BAND_LANES).astype(jnp.float32)
         here = (band_ref[0] + BAND_SHIFT).astype(jnp.float32)
         away_ref[...] = jnp.abs(jnp.transpose(bands) - here)
-
-    frames = slots_ref[:, :, :width].reshape(slots, width)
+        parts = width // FEATURES
+        own = lax.axis_index("tm") // (lax.axis_size("tm") // parts)
+        for part in range(parts):
+            start = pl.multiple_of(lax.rem(own + part, parts) * FEATURES, FEATURES)
+            frames_ref[:, part * FEATURES : (part + 1) * FEATURES] = slots_ref[
+                :, :, pl.ds(start, FEATURES)
+            ].reshape(slots, FEATURES)
+
+    frames = frames_ref[...]
     usable = away_ref[...] <= 1.0
     keys = jnp.dot(frames, wk_ref[...], preferred_element_type=jnp.float32).astype(jnp.bfloat16)
     values = jnp.dot(frames, wv_ref[...], preferred_element_type=jnp.float32).astype(jnp.bfloat16)
@@ -143,6 +153,7 @@
         scratch_shapes=[
             pltpu.VMEM((count, width), jnp.float32),
             pltpu.VMEM((count, slots.shape[0] * slots.shape[1]), jnp.float32),
+            pltpu.VMEM((slots.shape[0] * slots.shape[1], width), jnp.bfloat16),
         ],
         name="attend",
     )(
@@ -178,19 +189,53 @@
     groups = lax.axis_size("grp")
     capacity = max(2, 2 * local_rows // owners)
 
+    line = owners // LINES
+    half = groups // 2
+
+    late = lax.all_gather(
+        jnp.concatenate([up_weight, jnp.transpose(down_weight)], axis=0), "tm", axis=0, tiled=True
+    ).reshape(owners, 2, up_weight.shape[0], width)
+    up_rows = late[:, 0].reshape(width, width)
+    down_rows = late[:, 1].reshape(width, width)
+
+    shard = jnp.concatenate([kv_weight[:, :width], kv_weight[:, width:]], axis=0)
+    shard = (shard.astype(jnp.float32) * WEIGHT_SCALE).astype(jnp.float16)
+    fetched = []
+    for j in range(LINES // half):
+        pairs = []
+        for g in range(groups):
+            for source in range(LINES):
+                target = (source - (LINES // half) * (g % half) - j) % LINES
+                for k in range(line):
+                    pairs.append(
+                        (
+                            g * owners + source * line + k,
+                            g * owners + target * line + k,
+                        )
+                    )
+        fetched.append(lax.ppermute(shard, ("grp", "tm"), pairs))
+
     payload = pack(audio_rows, routing[:, 0], row_band, owners, capacity)
+    payload, fetched = lax.optimization_barrier((payload, jnp.concatenate(fetched, axis=0)))
     slots = lax.all_to_all(payload, "tm", split_axis=0, concat_axis=0, tiled=True)
-
-    shard = jnp.concatenate(
-        [kv_weight[:, :width], kv_weight[:, width:], up_weight, jnp.transpose(down_weight)], axis=0
-    )
-    shard = (shard.astype(jnp.float32) * WEIGHT_SCALE).astype(jnp.float16)
-    gathered = lax.all_gather(shard, "tm", axis=0, tiled=True)
-    gathered = gathered.reshape(owners, 4, kv_weight.shape[0], width)
+    lines = lax.all_gather(
+        fetched,
+        "grp",
+        axis=0,
+        tiled=True,
+        axis_index_groups=[list(range(h * half, (h + 1) * half)) for h in range(2)],
+    )
+    gathered = lax.all_gather(
+        lines,
+        "tm",
+        axis=0,
+        tiled=True,
+        axis_index_groups=[list(range(z * line, (z + 1) * line)) for z in range(LINES)],
+    ).reshape(line, LINES, 2, kv_weight.shape[0], width)
 
     def whole(index):
-        part = gathered[:, index].astype(jnp.float32) * (1.0 / WEIGHT_SCALE)
-        return part.astype(jnp.bfloat16).reshape(width, width)
+        part = jnp.transpose(gathered[:, :, index], (1, 0, 2, 3)).astype(jnp.float32)
+        return (part * (1.0 / WEIGHT_SCALE)).astype(jnp.bfloat16).reshape(width, width)
 
     joined = attend(
         slots, block_band, latents, whole(0), whole(1), null_key, null_value, out_weight
@@ -201,10 +246,9 @@
     center = values - jnp.mean(values, axis=-1, keepdims=True)
     spread = jnp.mean(center * center, axis=-1, keepdims=True)
     normed = (center * lax.rsqrt(spread + 1e-05) * mlp_gain).astype(jnp.bfloat16)
-    hidden = jax.nn.gelu(jnp.dot(normed, whole(2), preferred_element_type=jnp.float32)).astype(
+    hidden = jax.nn.gelu(jnp.dot(normed, up_rows, preferred_element_type=jnp.float32)).astype(
         jnp.bfloat16
     )
-    down_rows = whole(3)
     me = lax.axis_index("grp")
     columns = width // groups
 

time: 198 us -> 191 us (0.965)
  the two profiles are of different devices: /device:TPU:64 before, /device:TPU:2 now
where the time goes in v3:
time: 191 us; the launch traced here: 190 us
  blocking collectives  86.1 us (45%)
  starting transfers between devices  42.6 us (22%)
  between operations  14.3 us (7%)
  Pallas kernels  12.5 us (7%)
  waiting for transfers between devices  10.9 us (6%)
  matrix products  9.46 us (5%)
  other arithmetic  8.22 us (4%)
  local copies, waits for them, and re-layouts  6.19 us (3%)
    all_gather x1, blocking collectives, local(): window = lax.all_gather(sent, 'grp', axis=0, tiled=True)  35.9 us
    all_gather x1, blocking collectives, local(): lax.all_gather(lines, 'tm', axis=0, tiled=True, axis_index_groups=[list(r...  26.3 us
    ppermute x7, starting transfers between devices, hop(): return lax.ppermute(values, 'grp', pairs)  24.2 us
    all_gather x1, blocking collectives, local(): lax.all_gather(fetched, 'grp', axis=0, tiled=True, axis_index_groups=[lis...  23.8 us
    ppermute x2, starting transfers between devices, local(): fetched.append(lax.ppermute(shard, ('grp', 'tm'), pairs))  11.6 us
    ppermute x7, waiting for transfers between devices, hop(): return lax.ppermute(values, 'grp', pairs)  10.9 us
    pallas_call x1, Pallas kernels, attend(): pl.pallas_call(attend_kernel, grid=(width // step,), in_specs=[pl.BlockSp...  9.69 us
    all_to_all x1, starting transfers between devices, local(): lax.all_to_all(payload, 'tm', split_axis=0, concat_axis=0, tiled=True)  6.76 us
  transfers between devices with their start and end apart: 11, of which 5 were waited for; matrix products, arithmetic and copies ran while one was open for 7% of the time, Pallas kernels for 7%

profile of v3, /device:TPU:2, one launch (start us, length us, event | category | flops | bytes accessed | tf_op | source)
XLA Modules:
  0.0 190.3 jit_solution(2232671520889440308)
XLA Ops:
  6.5 1.4 pad_maximum_fusion.1
  7.9 0.0 all-gather.4.cloned.1.call-update
  8.0 0.8 fusion.42
  8.8 0.7 collective-permute-start
  9.4 10.9 %collective-permute-start.1 = (f16[32,1024]{1,0:T(8,128)(2,1)S(1)}, f16[32,1024]{1,0:T(8,128)(2,1)S(1)}, u32[]{:S(2)}, u32[]{:S(2)}) collective-permute-start(f16[32,1024]{1,0:T(8,128)(2,1)S(1)} %multiply_convert_fusion.7), channel_id=1, source_target_pairs={{0,56},{1,57},{2,58},{3,59},{4,60},{5,61},{6,62},{7,63},{8,0},{9,1... | collective-permute-start | bytes 196616 | tf_op jit(solution)/shard_map/ppermute | solution.py:216
  21.1 2.8 %pack.1 = bf16[64,8,1152]{2,1,0:T(8,128)(2,1)} custom-call(s32[1,256]{1,0:T(1,128)} %bitcast.44, s32[1,256]{1,0:T(1,128)} %bitcast.45, bf16[256,1024]{1,0:T(8,128)(2,1)} %refs_2_.1), custom_call_target="tpu_custom_call" | custom-call | tf_op jit(solution)/shard_map/pack/pallas_call | solution.py:57
  23.9 0.0 collective-permute-done
  24.0 6.8 %all-to-all-start = ((bf16[64,8,1152]{2,1,0:T(8,128)(2,1)}), bf16[64,8,1152]{2,1,0:T(8,128)(2,1)S(1)}, u32[]{:S(2)}, u32[]{:S(2)}) async-start(bf16[64,8,1152]{2,1,0:T(8,128)(2,1)} %pack.1), calls=%async_computation | async-start | bytes 2359296 | tf_op jit(solution)/shard_map/all_to_all | solution.py:220
  30.7 23.8 %all_gather.12 = f16[256,1024]{1,0:T(8,128)(2,1)S(1)} all-gather(f16[64,1024]{1,0:T(8,128)(2,1)S(1)} %pad_maximum_fusion), channel_id=1, replica_groups={{0,64,128,192},{256,320,384,448},{1,65,129,193},{257,321,385,449},{2,66..., dimensions={0}, use_global_device_ids=true | all-gather | bytes 655360 | tf_op jit(solution)/shard_map/all_gather | solution.py:221
  54.5 26.3 %all-gather.5 = f16[2048,1024]{1,0:T(8,128)(2,1)S(1)} all-gather(f16[256,1024]{1,0:T(8,128)(2,1)S(1)} %all_gather.12), channel_id=1, replica_groups={{0,1,2,3,4,5,6,7},{8,9,10,11,12,13,14,15},{16,17,18,19,20,21,22,23},{24..., dimensions={0}, use_global_device_ids=true | all-gather | bytes 4718592 | tf_op jit(solution)/shard_map/all_gather | solution.py:228
  80.9 1.6 fusion.41
  82.5 3.3 %multiply_convert_fusion.1 = (bf16[8,8,1,16,1024]{4,3,0,1,2:T(8,128)(2,1)}, bf16[8,8,1,16,1024]{4,3,0,1,2:T(8,128)(2,1)}) fusion(f16[8,8,1,16,1024]{4,3,2,1,0:T(8,128)(2,1)S(1)} %get-tuple-element.11, f16[8,8,1,16,1024]{4,3,2,1,0:T(8,128)(2,1)S(1)} %get-tuple-element.12), kind=kLoop, calls=%fused_computation.14 | loop fusion | flops 6291456 | bytes 8388608 | tf_op jit(solution)/shard_map/convert_element_type | solution.py:238
  85.8 1.1 copy-done
  86.9 9.7 %attend.1 = bf16[128,1024]{1,0:T(8,128)(2,1)} custom-call(s32[1]{0:T(128)S(6)} %copy.19.band_ref, bf16[64,8,1152]{2,1,0:T(8,128)(2,1)} %copy-done, bf16[128,1024]{1,0:T(8,128)(2,1)} %query_ref.1, bf16[128,1024]{1,0:T(8,128)(2,1)} %query_ref.1, bf16[1024,1024]{1,0:T(8,128)(2,1)} %bitcast.30, bf16[1024,1024]{1,0:T(8,128)(2,1)} %bitcast.29, ...), custom_call_target="tpu_custom_call" | custom-call | tf_op jit(solution)/shard_map/attend/pallas_call | solution.py:137
  96.6 1.0 multiply_convert_fusion.6
  97.7 35.9 %all-gather.6 = f16[1024,1024]{1,0:T(8,128)(2,1)S(1)} all-gather(f16[128,1024]{1,0:T(8,128)(2,1)S(1)} %multiply_convert_fusion.6), channel_id=1, replica_groups=mesh['grp'=8,'tm'=64] {'grp'}, dimensions={0}, use_global_device_ids=true | all-gather | bytes 2359296 | tf_op jit(solution)/shard_map/all_gather | solution.py:244
  133.6 0.5 fusion.9
  134.1 0.8 multiply_reduce_fusion
  134.9 0.0 all-gather.4.cloned.1.call-done
  134.9 0.0 copy-start.1
  134.9 2.7 %fusion.40 = (bf16[64,1,16,1024]{3,2,1,0:T(8,128)(2,1)S(1)}, bf16[64,1,16,1024]{3,2,1,0:T(8,128)(2,1)S(1)}) fusion(bf16[64,2,16,1024]{3,2,1,0:T(8,128)(2,1)} %bitcast.39), kind=kLoop, calls=%fused_computation.58 | loop fusion | bytes 8388608 | tf_op jit(solution)/shard_map/slice | solution.py:199
  137.6 3.7 %fusion.7 = bf16[1024,1024]{1,0:T(8,128)(2,1)S(1)} fusion(bf16[1024,1024]{1,0:T(8,128)(2,1)S(1)} %bitcast.40, f16[1024,1024]{1,0:T(8,128)(2,1)S(1)} %all-gather.6, f32[1024]{0:T(1024)S(1)} %copy-done.1, f32[1024]{0:T(1024)S(1)} %add_rsqrt_fusion, f32[1024]{0:T(1024)S(1)} %broadcast_multiply_fusion), kind=kOutput, calls=%fused_computation.8 | convolution fusion | flops 2163212288 | bytes 6303744 | tf_op jit(solution)/shard_map/dot_general | solution.py:249
  141.3 0.7 fusion.27
  142.1 2.2 %collective-permute-start.2 = (bf16[1024,128]{1,0:T(8,128)(2,1)S(1)}, bf16[1024,128]{1,0:T(8,128)(2,1)S(1)}, u32[]{:S(2)}, u32[]{:S(2)}) collective-permute-start(bf16[1024,128]{1,0:T(8,128)(2,1)S(1)} %fusion.27), channel_id=1, source_target_pairs={{0,64},{64,128},{128,192},{192,256},{256,320},{320,384},{384,448},... | collective-permute-start | bytes 786440 | tf_op jit(solution)/shard_map/ppermute | solution.py:267
  144.3 0.7 fusion.25
  145.0 0.7 fusion.23
  145.8 0.7 fusion.19
  146.5 5.0 %collective-permute-start.6 = (bf16[1024,128]{1,0:T(8,128)(2,1)S(1)}, bf16[1024,128]{1,0:T(8,128)(2,1)S(1)}, u32[]{:S(2)}, u32[]{:S(2)}) collective-permute-start(bf16[1024,128]{1,0:T(8,128)(2,1)S(1)} %fusion.19), channel_id=1, source_target_pairs={{0,448},{64,0},{128,64},{192,128},{256,192},{320,256},{384,320},{4... | collective-permute-start | bytes 786440 | tf_op jit(solution)/shard_map/ppermute | solution.py:267
  151.5 0.7 fusion.21
  152.2 0.1 add_convert_fusion.5
  152.3 1.9 %collective-permute-start.3 = (bf16[1024,128]{1,0:T(8,128)(2,1)S(1)}, bf16[1024,128]{1,0:T(8,128)(2,1)S(1)}, u32[]{:S(2)}, u32[]{:S(2)}) collective-permute-start(bf16[1024,128]{1,0:T(8,128)(2,1)S(1)} %add_convert_fusion.5), channel_id=1, source_target_pairs={{0,64},{64,128},{128,192},{192,256},{256,320},{320,384},{384,448},... | collective-permute-start | bytes 786440 | tf_op jit(solution)/shard_map/ppermute | solution.py:267
  154.2 0.7 fusion.17
  154.9 0.4 collective-permute-done.6
  155.4 0.1 add_convert_fusion.2
  155.4 5.6 %collective-permute-start.7 = (bf16[1024,128]{1,0:T(8,128)(2,1)S(1)}, bf16[1024,128]{1,0:T(8,128)(2,1)S(1)}, u32[]{:S(2)}, u32[]{:S(2)}) collective-permute-start(bf16[1024,128]{1,0:T(8,128)(2,1)S(1)} %add_convert_fusion.2), channel_id=1, source_target_pairs={{0,448},{64,0},{128,64},{192,128},{256,192},{320,256},{384,320},{4... | collective-permute-start | bytes 786440 | tf_op jit(solution)/shard_map/ppermute | solution.py:267
  161.1 1.0 collective-permute-done.3
  162.1 0.1 add_convert_fusion.4
  162.1 1.9 %collective-permute-start.4 = (bf16[1024,128]{1,0:T(8,128)(2,1)S(1)}, bf16[1024,128]{1,0:T(8,128)(2,1)S(1)}, u32[]{:S(2)}, u32[]{:S(2)}) collective-permute-start(bf16[1024,128]{1,0:T(8,128)(2,1)S(1)} %add_convert_fusion.4), channel_id=1, source_target_pairs={{0,64},{64,128},{128,192},{192,256},{256,320},{320,384},{384,448},... | collective-permute-start | bytes 786440 | tf_op jit(solution)/shard_map/ppermute | solution.py:267
  164.1 0.7 fusion.15
  164.8 1.3 collective-permute-done.7
  166.1 0.1 add_convert_fusion.1
  166.2 5.6 %collective-permute-start.8 = (bf16[1024,128]{1,0:T(8,128)(2,1)S(1)}, bf16[1024,128]{1,0:T(8,128)(2,1)S(1)}, u32[]{:S(2)}, u32[]{:S(2)}) collective-permute-start(bf16[1024,128]{1,0:T(8,128)(2,1)S(1)} %add_convert_fusion.1), channel_id=1, source_target_pairs={{0,448},{64,0},{128,64},{192,128},{256,192},{320,256},{384,320},{4... | collective-permute-start | bytes 786440 | tf_op jit(solution)/shard_map/ppermute | solution.py:267
  171.8 1.3 collective-permute-done.4
  173.1 0.1 add_convert_fusion.3
  173.1 1.9 %collective-permute-start.5 = (bf16[1024,128]{1,0:T(8,128)(2,1)S(1)}, bf16[1024,128]{1,0:T(8,128)(2,1)S(1)}, u32[]{:S(2)}, u32[]{:S(2)}) collective-permute-start(bf16[1024,128]{1,0:T(8,128)(2,1)S(1)} %add_convert_fusion.3), channel_id=1, source_target_pairs={{0,64},{64,128},{128,192},{192,256},{256,320},{320,384},{384,448},... | collective-permute-start | bytes 786440 | tf_op jit(solution)/shard_map/ppermute | solution.py:267
  175.0 0.7 fusion.29
  175.8 6.8 %collective-permute-done.5 = bf16[1024,128]{1,0:T(8,128)(2,1)S(1)} collective-permute-done((bf16[1024,128]{1,0:T(8,128)(2,1)S(1)}, bf16[1024,128]{1,0:T(8,128)(2,1)S(1)}, u32[]{:S(2)}, u32[]{:S(2)}) %collective-permute-start.5) | collective-permute-done | bytes 262176 | tf_op jit(solution)/shard_map/ppermute | solution.py:267
  182.6 0.9 add_convert_fusion
  (11 shorter events, 0.1 us)
Async XLA Ops:
  6.5 128.3 %all-gather.4.cloned.1.call-start = ((), (), s32[]{:S(2)}) async-start(), calls=%async_computation.1 | async-start | bytes 4259840 | tf_op jit(solution)/shard_map/all_gather | solution.py:195
  8.8 15.2 %collective-permute-start = (f16[32,1024]{1,0:T(8,128)(2,1)S(1)}, f16[32,1024]{1,0:T(8,128)(2,1)S(1)}, u32[]{:S(2)}, u32[]{:S(2)}) collective-permute-start(f16[32,1024]{1,0:T(8,128)(2,1)S(1)} %multiply_convert_fusion.7), channel_id=1, source_target_pairs={{0,0},{1,1},{2,2},{3,3},{4,4},{5,5},{6,6},{7,7},{8,8},{9,9},{10,10... | collective-permute-start | bytes 196616 | tf_op jit(solution)/shard_map/ppermute | solution.py:216
  9.4 14.5 %collective-permute-start.1 = (f16[32,1024]{1,0:T(8,128)(2,1)S(1)}, f16[32,1024]{1,0:T(8,128)(2,1)S(1)}, u32[]{:S(2)}, u32[]{:S(2)}) collective-permute-start(f16[32,1024]{1,0:T(8,128)(2,1)S(1)} %multiply_convert_fusion.7), channel_id=1, source_target_pairs={{0,56},{1,57},{2,58},{3,59},{4,60},{5,61},{6,62},{7,63},{8,0},{9,1... | collective-permute-start | bytes 196616 | tf_op jit(solution)/shard_map/ppermute | solution.py:216
  24.0 61.9 %all-to-all-start = ((bf16[64,8,1152]{2,1,0:T(8,128)(2,1)}), bf16[64,8,1152]{2,1,0:T(8,128)(2,1)S(1)}, u32[]{:S(2)}, u32[]{:S(2)}) async-start(bf16[64,8,1152]{2,1,0:T(8,128)(2,1)} %pack.1), calls=%async_computation | async-start | bytes 2359296 | tf_op jit(solution)/shard_map/all_to_all | solution.py:220
  85.8 1.1 copy-start
  134.9 2.7 %copy-start.1 = (f32[1024]{0:T(1024)S(1)}, f32[1024]{0:T(1024)}, u32[]{:S(2)}) copy-start(f32[1024]{0:T(1024)} %param.21) | copy-start | bytes 12292
  142.1 10.1 %collective-permute-start.2 = (bf16[1024,128]{1,0:T(8,128)(2,1)S(1)}, bf16[1024,128]{1,0:T(8,128)(2,1)S(1)}, u32[]{:S(2)}, u32[]{:S(2)}) collective-permute-start(bf16[1024,128]{1,0:T(8,128)(2,1)S(1)} %fusion.27), channel_id=1, source_target_pairs={{0,64},{64,128},{128,192},{192,256},{256,320},{320,384},{384,448},... | collective-permute-start | bytes 786440 | tf_op jit(solution)/shard_map/ppermute | solution.py:267
  146.5 8.9 %collective-permute-start.6 = (bf16[1024,128]{1,0:T(8,128)(2,1)S(1)}, bf16[1024,128]{1,0:T(8,128)(2,1)S(1)}, u32[]{:S(2)}, u32[]{:S(2)}) collective-permute-start(bf16[1024,128]{1,0:T(8,128)(2,1)S(1)} %fusion.19), channel_id=1, source_target_pairs={{0,448},{64,0},{128,64},{192,128},{256,192},{320,256},{384,320},{4... | collective-permute-start | bytes 786440 | tf_op jit(solution)/shard_map/ppermute | solution.py:267
  152.3 9.8 %collective-permute-start.3 = (bf16[1024,128]{1,0:T(8,128)(2,1)S(1)}, bf16[1024,128]{1,0:T(8,128)(2,1)S(1)}, u32[]{:S(2)}, u32[]{:S(2)}) collective-permute-start(bf16[1024,128]{1,0:T(8,128)(2,1)S(1)} %add_convert_fusion.5), channel_id=1, source_target_pairs={{0,64},{64,128},{128,192},{192,256},{256,320},{320,384},{384,448},... | collective-permute-start | bytes 786440 | tf_op jit(solution)/shard_map/ppermute | solution.py:267
  155.4 10.7 %collective-permute-start.7 = (bf16[1024,128]{1,0:T(8,128)(2,1)S(1)}, bf16[1024,128]{1,0:T(8,128)(2,1)S(1)}, u32[]{:S(2)}, u32[]{:S(2)}) collective-permute-start(bf16[1024,128]{1,0:T(8,128)(2,1)S(1)} %add_convert_fusion.2), channel_id=1, source_target_pairs={{0,448},{64,0},{128,64},{192,128},{256,192},{320,256},{384,320},{4... | collective-permute-start | bytes 786440 | tf_op jit(solution)/shard_map/ppermute | solution.py:267
  162.1 10.9 %collective-permute-start.4 = (bf16[1024,128]{1,0:T(8,128)(2,1)S(1)}, bf16[1024,128]{1,0:T(8,128)(2,1)S(1)}, u32[]{:S(2)}, u32[]{:S(2)}) collective-permute-start(bf16[1024,128]{1,0:T(8,128)(2,1)S(1)} %add_convert_fusion.4), channel_id=1, source_target_pairs={{0,64},{64,128},{128,192},{192,256},{256,320},{320,384},{384,448},... | collective-permute-start | bytes 786440 | tf_op jit(solution)/shard_map/ppermute | solution.py:267
  166.2 9.6 %collective-permute-start.8 = (bf16[1024,128]{1,0:T(8,128)(2,1)S(1)}, bf16[1024,128]{1,0:T(8,128)(2,1)S(1)}, u32[]{:S(2)}, u32[]{:S(2)}) collective-permute-start(bf16[1024,128]{1,0:T(8,128)(2,1)S(1)} %add_convert_fusion.1), channel_id=1, source_target_pairs={{0,448},{64,0},{128,64},{192,128},{256,192},{320,256},{384,320},{4... | collective-permute-start | bytes 786440 | tf_op jit(solution)/shard_map/ppermute | solution.py:267
  173.1 9.5 %collective-permute-start.5 = (bf16[1024,128]{1,0:T(8,128)(2,1)S(1)}, bf16[1024,128]{1,0:T(8,128)(2,1)S(1)}, u32[]{:S(2)}, u32[]{:S(2)}) collective-permute-start(bf16[1024,128]{1,0:T(8,128)(2,1)S(1)} %add_convert_fusion.3), channel_id=1, source_target_pairs={{0,64},{64,128},{128,192},{192,256},{256,320},{320,384},{384,448},... | collective-permute-start | bytes 786440 | tf_op jit(solution)/shard_map/ppermute | solution.py:267
Sparse Core Ops, SparseCore 0:
  10.7 91.4 all-gather.3

commit v4 on v3

--- a/solution.py
+++ b/solution.py
@@ -97,10 +97,16 @@
 
     frames = frames_ref[...]
     usable = away_ref[...] <= 1.0
-    keys = jnp.dot(frames, wk_ref[...], preferred_element_type=jnp.float32).astype(jnp.bfloat16)
-    values = jnp.dot(frames, wv_ref[...], preferred_element_type=jnp.float32).astype(jnp.bfloat16)
+
+    def rows_of(ref):
+        return jnp.concatenate(
+            [ref[:, part].reshape(FEATURES, ref.shape[3]) for part in range(ref.shape[1])], axis=0
+        )
+
+    keys = jnp.dot(frames, rows_of(wk_ref), preferred_element_type=jnp.float32).astype(jnp.bfloat16)
+    values = jnp.dot(frames, rows_of(wv_ref), preferred_element_type=jnp.float32).astype(jnp.bfloat16)
     attended = []
-    for h in range(wk_ref.shape[1] // HD):
+    for h in range(wk_ref.shape[3] // HD):
         cols = slice(h * HD, (h + 1) * HD)
         query = query_ref[:, cols]
         score = (
@@ -131,7 +137,7 @@
         out_ref[...] = acc_ref[...].astype(jnp.bfloat16)
 
 
-def attend(slots, block_band, latents, wk, wv, null_key, null_value, out_weight):
+def attend(slots, block_band, latents, kv, null_key, null_value, out_weight):
     count, width = latents.shape
     step = 4 * HD
     return pl.pallas_call(
@@ -142,8 +148,8 @@
             pl.BlockSpec(slots.shape, lambda i: (0, 0, 0)),
             pl.BlockSpec((count, width), lambda i: (0, 0)),
             pl.BlockSpec((count, step), lambda i: (0, i)),
-            pl.BlockSpec((width, step), lambda i: (0, i)),
-            pl.BlockSpec((width, step), lambda i: (0, i)),
+            pl.BlockSpec((*kv.shape[:2], None, kv.shape[3], step), lambda i: (0, 0, 0, 0, i)),
+            pl.BlockSpec((*kv.shape[:2], None, kv.shape[3], step), lambda i: (0, 0, 1, 0, i)),
             pl.BlockSpec((1, step), lambda i: (0, i)),
             pl.BlockSpec((1, step), lambda i: (0, i)),
             pl.BlockSpec((step, width), lambda i: (i, 0)),
@@ -161,8 +167,8 @@
         slots,
         latents,
         latents,
-        wk,
-        wv,
+        kv,
+        kv,
         null_key.reshape(1, width),
         null_value.reshape(1, width),
         out_weight,
@@ -190,7 +196,6 @@
     capacity = max(2, 2 * local_rows // owners)
 
     line = owners // LINES
-    half = groups // 2
 
     late = lax.all_gather(
         jnp.concatenate([up_weight, jnp.transpose(down_weight)], axis=0), "tm", axis=0, tiled=True
@@ -200,46 +205,24 @@
 
     shard = jnp.concatenate([kv_weight[:, :width], kv_weight[:, width:]], axis=0)
     shard = (shard.astype(jnp.float32) * WEIGHT_SCALE).astype(jnp.float16)
-    fetched = []
-    for j in range(LINES // half):
-        pairs = []
-        for g in range(groups):
-            for source in range(LINES):
-                target = (source - (LINES // half) * (g % half) - j) % LINES
-                for k in range(line):
-                    pairs.append(
-                        (
-                            g * owners + source * line + k,
-                            g * owners + target * line + k,
-                        )
-                    )
-        fetched.append(lax.ppermute(shard, ("grp", "tm"), pairs))
+    fetched = [shard]
+    for shift in range(1, LINES):
+        pairs = [(i, (i - shift * line) % owners) for i in range(owners)]
+        fetched.append(lax.ppermute(shard, "tm", pairs))
 
     payload = pack(audio_rows, routing[:, 0], row_band, owners, capacity)
-    payload, fetched = lax.optimization_barrier((payload, jnp.concatenate(fetched, axis=0)))
     slots = lax.all_to_all(payload, "tm", split_axis=0, concat_axis=0, tiled=True)
-    lines = lax.all_gather(
-        fetched,
-        "grp",
-        axis=0,
-        tiled=True,
-        axis_index_groups=[list(range(h * half, (h + 1) * half)) for h in range(2)],
-    )
     gathered = lax.all_gather(
-        lines,
+        jnp.concatenate(fetched, axis=0),
         "tm",
         axis=0,
         tiled=True,
         axis_index_groups=[list(range(z * line, (z + 1) * line)) for z in range(LINES)],
-    ).reshape(line, LINES, 2, kv_weight.shape[0], width)
-
-    def whole(index):
-        part = jnp.transpose(gathered[:, :, index], (1, 0, 2, 3)).astype(jnp.float32)
-        return (part * (1.0 / WEIGHT_SCALE)).astype(jnp.bfloat16).reshape(width, width)
-
-    joined = attend(
-        slots, block_band, latents, whole(0), whole(1), null_key, null_value, out_weight
-    )
+    )
+    kv = (gathered.astype(jnp.float32) * (1.0 / WEIGHT_SCALE)).astype(jnp.bfloat16)
+    kv = kv.reshape(line, LINES, 2, kv_weight.shape[0], width)
+
+    joined = attend(slots, block_band, latents, kv, null_key, null_value, out_weight)
     sent = (joined.astype(jnp.float32) * JOINED_SCALE).astype(jnp.float16)
     window = lax.all_gather(sent, "grp", axis=0, tiled=True)
     values = window.astype(jnp.float32) * (1.0 / JOINED_SCALE)

time: 191 us -> 213 us (1.12)
  blocking collectives: 86.1 us -> 55.2 us
  waiting for transfers between devices: 10.9 us -> 41.4 us
  starting transfers between devices: 42.6 us -> 66.8 us
    ppermute x2 -> x7, waiting for transfers between devices: 0.01 us -> 28.1 us  [local(): fetched.append(lax.ppermute(shard, 'tm', pairs))]
    all_gather x2 -> x1, blocking collectives: 50.1 us -> 23.7 us  [local(): lax.all_gather(jnp.concatenate(fetched, axis=0), 'tm', axis=0, tiled=True...]
    ppermute x2 -> x7, starting transfers between devices: 11.6 us -> 32.8 us  [local(): fetched.append(lax.ppermute(shard, 'tm', pairs))]
    all_gather x1, blocking collectives: 35.9 us -> 31.5 us  [local(): window = lax.all_gather(sent, 'grp', axis=0, tiled=True)]
    all_to_all x1, starting transfers between devices: 6.76 us -> 9.87 us  [local(): lax.all_to_all(payload, 'tm', split_axis=0, concat_axis=0, tiled=True)]
    ppermute x7, waiting for transfers between devices: 10.9 us -> 13.2 us  [hop(): return lax.ppermute(values, 'grp', pairs)]
  transfers between devices with their start and end apart: 11 -> 16, of which waited for: 5 -> 7; matrix products, arithmetic and copies ran while one was open for 7% -> 6% of each run, Pallas kernels for 7% -> 6%
where the time goes in v4:
time: 213 us; the launch traced here: 212 us
  starting transfers between devices  66.8 us (31%)
  blocking collectives  55.2 us (26%)
  waiting for transfers between devices  41.4 us (19%)
  between operations  14.4 us (7%)
  Pallas kernels  12.1 us (6%)
  matrix products  9.46 us (4%)
  other arithmetic  8.11 us (4%)
  local copies, waits for them, and re-layouts  4.7 us (2%)
    ppermute x7, starting transfers between devices, local(): fetched.append(lax.ppermute(shard, 'tm', pairs))  32.8 us
    all_gather x1, blocking collectives, local(): window = lax.all_gather(sent, 'grp', axis=0, tiled=True)  31.5 us
    ppermute x7, waiting for transfers between devices, local(): fetched.append(lax.ppermute(shard, 'tm', pairs))  28.1 us
    ppermute x7, starting transfers between devices, hop(): return lax.ppermute(values, 'grp', pairs)  24.2 us
    all_gather x1, blocking collectives, local(): lax.all_gather(jnp.concatenate(fetched, axis=0), 'tm', axis=0, tiled=True...  23.7 us
    ppermute x7, waiting for transfers between devices, hop(): return lax.ppermute(values, 'grp', pairs)  13.2 us
    all_to_all x1, starting transfers between devices, local(): lax.all_to_all(payload, 'tm', split_axis=0, concat_axis=0, tiled=True)  9.87 us
    pallas_call x1, Pallas kernels, attend(): pl.pallas_call(attend_kernel, grid=(width // step,), in_specs=[pl.BlockSp...  9.28 us
  transfers between devices with their start and end apart: 16, of which 7 were waited for; matrix products, arithmetic and copies ran while one was open for 6% of the time, Pallas kernels for 6%

profile of v4, /device:TPU:2, one launch (start us, length us, event | category | flops | bytes accessed | tf_op | source)
XLA Modules:
  0.0 212.2 jit_solution(10841224589276063851)
XLA Ops:
  6.5 1.4 pad_maximum_fusion
  8.0 0.8 fusion.41
  8.8 10.9 %collective-permute-start = (f16[32,1024]{1,0:T(8,128)(2,1)S(1)}, f16[32,1024]{1,0:T(8,128)(2,1)S(1)}, u32[]{:S(2)}, u32[]{:S(2)}) collective-permute-start(f16[32,1024]{1,0:T(8,128)(2,1)S(1)} %multiply_convert_fusion.6), channel_id=1, source_target_pairs={{0,56},{1,57},{2,58},{3,59},{4,60},{5,61},{6,62},{7,63},{8,0},{9,1... | collective-permute-start | bytes 196616 | tf_op jit(solution)/shard_map/ppermute | solution.py:211
  19.7 2.5 %collective-permute-start.1 = (f16[32,1024]{1,0:T(8,128)(2,1)S(1)}, f16[32,1024]{1,0:T(8,128)(2,1)S(1)}, u32[]{:S(2)}, u32[]{:S(2)}) collective-permute-start(f16[32,1024]{1,0:T(8,128)(2,1)S(1)} %multiply_convert_fusion.6), channel_id=1, source_target_pairs={{0,48},{1,49},{2,50},{3,51},{4,52},{5,53},{6,54},{7,55},{8,56},{9,... | collective-permute-start | bytes 196616 | tf_op jit(solution)/shard_map/ppermute | solution.py:211
  22.2 1.9 collective-permute-start.2
  24.1 7.8 %collective-permute-start.3 = (f16[32,1024]{1,0:T(8,128)(2,1)S(1)}, f16[32,1024]{1,0:T(8,128)(2,1)S(1)}, u32[]{:S(2)}, u32[]{:S(2)}) collective-permute-start(f16[32,1024]{1,0:T(8,128)(2,1)S(1)} %multiply_convert_fusion.6), channel_id=1, source_target_pairs={{0,32},{1,33},{2,34},{3,35},{4,36},{5,37},{6,38},{7,39},{8,40},{9,... | collective-permute-start | bytes 196616 | tf_op jit(solution)/shard_map/ppermute | solution.py:211
  32.0 1.9 collective-permute-start.4
  33.9 2.8 %pack.1 = bf16[64,8,1152]{2,1,0:T(8,128)(2,1)} custom-call(s32[1,256]{1,0:T(1,128)} %bitcast.33, s32[1,256]{1,0:T(1,128)} %bitcast.34, bf16[256,1024]{1,0:T(8,128)(2,1)} %refs_2_.1), custom_call_target="tpu_custom_call" | custom-call | tf_op jit(solution)/shard_map/pack/pallas_call | solution.py:57
  36.7 9.9 %all-to-all-start = ((bf16[64,8,1152]{2,1,0:T(8,128)(2,1)}), bf16[64,8,1152]{2,1,0:T(8,128)(2,1)S(1)}, u32[]{:S(2)}, u32[]{:S(2)}) async-start(bf16[64,8,1152]{2,1,0:T(8,128)(2,1)} %pack.1), calls=%async_computation | async-start | bytes 2359296 | tf_op jit(solution)/shard_map/all_to_all | solution.py:214
  47.3 4.3 %collective-permute-start.5 = (f16[32,1024]{1,0:T(8,128)(2,1)S(1)}, f16[32,1024]{1,0:T(8,128)(2,1)S(1)}, u32[]{:S(2)}, u32[]{:S(2)}) collective-permute-start(f16[32,1024]{1,0:T(8,128)(2,1)S(1)} %multiply_convert_fusion.6), channel_id=1, source_target_pairs={{0,16},{1,17},{2,18},{3,19},{4,20},{5,21},{6,22},{7,23},{8,24},{9,... | collective-permute-start | bytes 196616 | tf_op jit(solution)/shard_map/ppermute | solution.py:211
  51.7 3.4 %collective-permute-start.6 = (f16[32,1024]{1,0:T(8,128)(2,1)S(1)}, f16[32,1024]{1,0:T(8,128)(2,1)S(1)}, u32[]{:S(2)}, u32[]{:S(2)}) collective-permute-start(f16[32,1024]{1,0:T(8,128)(2,1)S(1)} %multiply_convert_fusion.6), channel_id=1, source_target_pairs={{0,8},{1,9},{2,10},{3,11},{4,12},{5,13},{6,14},{7,15},{8,16},{9,17... | collective-permute-start | bytes 196616 | tf_op jit(solution)/shard_map/ppermute | solution.py:211
  55.2 27.4 %collective-permute-done.5 = f16[32,1024]{1,0:T(8,128)(2,1)S(1)} collective-permute-done((f16[32,1024]{1,0:T(8,128)(2,1)S(1)}, f16[32,1024]{1,0:T(8,128)(2,1)S(1)}, u32[]{:S(2)}, u32[]{:S(2)}) %collective-permute-start.5) | collective-permute-done | bytes 65568 | tf_op jit(solution)/shard_map/ppermute | solution.py:211
  82.6 0.7 collective-permute-done.6
  83.3 23.7 %all-gather.5 = f16[2048,1024]{1,0:T(8,128)(2,1)S(1)} all-gather(f16[256,1024]{1,0:T(8,128)(2,1)S(1)} %constant_dynamic-update-slice_fusion), channel_id=1, replica_groups={{0,1,2,3,4,5,6,7},{8,9,10,11,12,13,14,15},{16,17,18,19,20,21,22,23},{24..., dimensions={0}, use_global_device_ids=true | all-gather | bytes 4718592 | tf_op jit(solution)/shard_map/all_gather | solution.py:215
  107.1 3.2 %multiply_convert_fusion = bf16[2048,1024]{1,0:T(8,128)(2,1)} fusion(f16[2048,1024]{1,0:T(8,128)(2,1)S(1)} %all-gather.5), kind=kLoop, calls=%fused_computation | loop fusion | flops 6291456 | bytes 8388608 | tf_op jit(solution)/shard_map/convert_element_type | solution.py:222
  110.3 1.1 copy-done
  111.4 9.3 %attend.1 = bf16[128,1024]{1,0:T(8,128)(2,1)} custom-call(s32[1]{0:T(128)S(6)} %copy.20.band_ref, bf16[64,8,1152]{2,1,0:T(8,128)(2,1)} %copy-done, bf16[128,1024]{1,0:T(8,128)(2,1)} %query_ref.1, bf16[128,1024]{1,0:T(8,128)(2,1)} %query_ref.1, bf16[8,8,2,16,1024]{4,3,2,1,0:T(8,128)(2,1)} %bitcast.18, bf16[8,8,2,16,1024]{4,3,2,1,0:T(8,128)(2,1)} %bitcast.19, ...), custom_call_target="tpu_custom_call" | custom-call | tf_op jit(solution)/shard_map/attend/pallas_call | solution.py:143
  120.7 1.0 multiply_convert_fusion.5
  121.7 31.5 %all-gather.6 = f16[1024,1024]{1,0:T(8,128)(2,1)S(1)} all-gather(f16[128,1024]{1,0:T(8,128)(2,1)S(1)} %multiply_convert_fusion.5), channel_id=1, replica_groups=mesh['grp'=8,'tm'=64] {'grp'}, dimensions={0}, use_global_device_ids=true | all-gather | bytes 2359296 | tf_op jit(solution)/shard_map/all_gather | solution.py:227
  153.2 0.5 fusion.9
  153.7 0.8 multiply_reduce_fusion
  154.5 2.7 %fusion.40 = (bf16[64,1,16,1024]{3,2,1,0:T(8,128)(2,1)S(1)}, bf16[64,1,16,1024]{3,2,1,0:T(8,128)(2,1)S(1)}) fusion(bf16[64,2,16,1024]{3,2,1,0:T(8,128)(2,1)} %bitcast.28), kind=kLoop, calls=%fused_computation.64 | loop fusion | bytes 8388608 | tf_op jit(solution)/shard_map/slice | solution.py:204
  157.2 3.7 %fusion.7 = bf16[1024,1024]{1,0:T(8,128)(2,1)S(1)} fusion(bf16[1024,1024]{1,0:T(8,128)(2,1)S(1)} %bitcast.29, f16[1024,1024]{1,0:T(8,128)(2,1)S(1)} %all-gather.6, f32[1024]{0:T(1024)S(1)} %copy-done.1, f32[1024]{0:T(1024)S(1)} %add_rsqrt_fusion, f32[1024]{0:T(1024)S(1)} %broadcast_multiply_fusion), kind=kOutput, calls=%fused_computation.9 | convolution fusion | flops 2163212288 | bytes 6303744 | tf_op jit(solution)/shard_map/dot_general | solution.py:232
  161.0 0.7 fusion.27
  161.7 2.8 %collective-permute-start.7 = (bf16[1024,128]{1,0:T(8,128)(2,1)S(1)}, bf16[1024,128]{1,0:T(8,128)(2,1)S(1)}, u32[]{:S(2)}, u32[]{:S(2)}) collective-permute-start(bf16[1024,128]{1,0:T(8,128)(2,1)S(1)} %fusion.27), channel_id=1, source_target_pairs={{0,64},{64,128},{128,192},{192,256},{256,320},{320,384},{384,448},... | collective-permute-start | bytes 786440 | tf_op jit(solution)/shard_map/ppermute | solution.py:250
  164.5 0.7 fusion.25
  165.2 0.7 fusion.23
  165.9 0.7 fusion.19
  166.7 4.4 %collective-permute-start.11 = (bf16[1024,128]{1,0:T(8,128)(2,1)S(1)}, bf16[1024,128]{1,0:T(8,128)(2,1)S(1)}, u32[]{:S(2)}, u32[]{:S(2)}) collective-permute-start(bf16[1024,128]{1,0:T(8,128)(2,1)S(1)} %fusion.19), channel_id=1, source_target_pairs={{0,448},{64,0},{128,64},{192,128},{256,192},{320,256},{384,320},{4... | collective-permute-start | bytes 786440 | tf_op jit(solution)/shard_map/ppermute | solution.py:250
  171.1 0.7 fusion.21
  171.8 0.1 add_convert_fusion.5
  171.9 1.9 collective-permute-start.8
  173.8 0.7 fusion.17
  174.5 1.6 collective-permute-done.11
  176.2 5.6 %collective-permute-start.12 = (bf16[1024,128]{1,0:T(8,128)(2,1)S(1)}, bf16[1024,128]{1,0:T(8,128)(2,1)S(1)}, u32[]{:S(2)}, u32[]{:S(2)}) collective-permute-start(bf16[1024,128]{1,0:T(8,128)(2,1)S(1)} %add_convert_fusion.2), channel_id=1, source_target_pairs={{0,448},{64,0},{128,64},{192,128},{256,192},{320,256},{384,320},{4... | collective-permute-start | bytes 786440 | tf_op jit(solution)/shard_map/ppermute | solution.py:250
  181.8 1.0 collective-permute-done.8
  182.8 0.1 add_convert_fusion.4
  182.9 1.9 collective-permute-start.9
  184.8 0.7 fusion.15
  185.5 2.5 %collective-permute-done.12 = bf16[1024,128]{1,0:T(8,128)(2,1)S(1)} collective-permute-done((bf16[1024,128]{1,0:T(8,128)(2,1)S(1)}, bf16[1024,128]{1,0:T(8,128)(2,1)S(1)}, u32[]{:S(2)}, u32[]{:S(2)}) %collective-permute-start.12) | collective-permute-done | bytes 262176 | tf_op jit(solution)/shard_map/ppermute | solution.py:250
  188.0 0.1 add_convert_fusion.1
  188.1 5.6 %collective-permute-start.13 = (bf16[1024,128]{1,0:T(8,128)(2,1)S(1)}, bf16[1024,128]{1,0:T(8,128)(2,1)S(1)}, u32[]{:S(2)}, u32[]{:S(2)}) collective-permute-start(bf16[1024,128]{1,0:T(8,128)(2,1)S(1)} %add_convert_fusion.1), channel_id=1, source_target_pairs={{0,448},{64,0},{128,64},{192,128},{256,192},{320,256},{384,320},{4... | collective-permute-start | bytes 786440 | tf_op jit(solution)/shard_map/ppermute | solution.py:250
  193.7 1.3 collective-permute-done.9
  195.0 0.1 add_convert_fusion.3
  195.1 1.9 collective-permute-start.10
  197.0 0.7 fusion.29
  197.7 6.8 %collective-permute-done.10 = bf16[1024,128]{1,0:T(8,128)(2,1)S(1)} collective-permute-done((bf16[1024,128]{1,0:T(8,128)(2,1)S(1)}, bf16[1024,128]{1,0:T(8,128)(2,1)S(1)}, u32[]{:S(2)}, u32[]{:S(2)}) %collective-permute-start.10) | collective-permute-done | bytes 262176 | tf_op jit(solution)/shard_map/ppermute | solution.py:250
  204.5 0.8 add_convert_fusion
  (26 shorter events, 0.3 us)
Async XLA Ops:
  6.5 148.0 %all-gather.4.cloned.1.call-start = ((), (), s32[]{:S(2)}) async-start(), calls=%async_computation.1 | async-start | bytes 4259840 | tf_op jit(solution)/shard_map/all_gather | solution.py:200
  8.8 38.6 %collective-permute-start = (f16[32,1024]{1,0:T(8,128)(2,1)S(1)}, f16[32,1024]{1,0:T(8,128)(2,1)S(1)}, u32[]{:S(2)}, u32[]{:S(2)}) collective-permute-start(f16[32,1024]{1,0:T(8,128)(2,1)S(1)} %multiply_convert_fusion.6), channel_id=1, source_target_pairs={{0,56},{1,57},{2,58},{3,59},{4,60},{5,61},{6,62},{7,63},{8,0},{9,1... | collective-permute-start | bytes 196616 | tf_op jit(solution)/shard_map/ppermute | solution.py:211
  19.7 31.9 %collective-permute-start.1 = (f16[32,1024]{1,0:T(8,128)(2,1)S(1)}, f16[32,1024]{1,0:T(8,128)(2,1)S(1)}, u32[]{:S(2)}, u32[]{:S(2)}) collective-permute-start(f16[32,1024]{1,0:T(8,128)(2,1)S(1)} %multiply_convert_fusion.6), channel_id=1, source_target_pairs={{0,48},{1,49},{2,50},{3,51},{4,52},{5,53},{6,54},{7,55},{8,56},{9,... | collective-permute-start | bytes 196616 | tf_op jit(solution)/shard_map/ppermute | solution.py:211
  22.2 32.9 %collective-permute-start.2 = (f16[32,1024]{1,0:T(8,128)(2,1)S(1)}, f16[32,1024]{1,0:T(8,128)(2,1)S(1)}, u32[]{:S(2)}, u32[]{:S(2)}) collective-permute-start(f16[32,1024]{1,0:T(8,128)(2,1)S(1)} %multiply_convert_fusion.6), channel_id=1, source_target_pairs={{0,40},{1,41},{2,42},{3,43},{4,44},{5,45},{6,46},{7,47},{8,48},{9,... | collective-permute-start | bytes 196616 | tf_op jit(solution)/shard_map/ppermute | solution.py:211
  24.1 31.0 %collective-permute-start.3 = (f16[32,1024]{1,0:T(8,128)(2,1)S(1)}, f16[32,1024]{1,0:T(8,128)(2,1)S(1)}, u32[]{:S(2)}, u32[]{:S(2)}) collective-permute-start(f16[32,1024]{1,0:T(8,128)(2,1)S(1)} %multiply_convert_fusion.6), channel_id=1, source_target_pairs={{0,32},{1,33},{2,34},{3,35},{4,36},{5,37},{6,38},{7,39},{8,40},{9,... | collective-permute-start | bytes 196616 | tf_op jit(solution)/shard_map/ppermute | solution.py:211
  32.0 23.2 %collective-permute-start.4 = (f16[32,1024]{1,0:T(8,128)(2,1)S(1)}, f16[32,1024]{1,0:T(8,128)(2,1)S(1)}, u32[]{:S(2)}, u32[]{:S(2)}) collective-permute-start(f16[32,1024]{1,0:T(8,128)(2,1)S(1)} %multiply_convert_fusion.6), channel_id=1, source_target_pairs={{0,24},{1,25},{2,26},{3,27},{4,28},{5,29},{6,30},{7,31},{8,32},{9,... | collective-permute-start | bytes 196616 | tf_op jit(solution)/shard_map/ppermute | solution.py:211
  36.7 73.6 %all-to-all-start = ((bf16[64,8,1152]{2,1,0:T(8,128)(2,1)}), bf16[64,8,1152]{2,1,0:T(8,128)(2,1)S(1)}, u32[]{:S(2)}, u32[]{:S(2)}) async-start(bf16[64,8,1152]{2,1,0:T(8,128)(2,1)} %pack.1), calls=%async_computation | async-start | bytes 2359296 | tf_op jit(solution)/shard_map/all_to_all | solution.py:214
  47.3 35.3 %collective-permute-start.5 = (f16[32,1024]{1,0:T(8,128)(2,1)S(1)}, f16[32,1024]{1,0:T(8,128)(2,1)S(1)}, u32[]{:S(2)}, u32[]{:S(2)}) collective-permute-start(f16[32,1024]{1,0:T(8,128)(2,1)S(1)} %multiply_convert_fusion.6), channel_id=1, source_target_pairs={{0,16},{1,17},{2,18},{3,19},{4,20},{5,21},{6,22},{7,23},{8,24},{9,... | collective-permute-start | bytes 196616 | tf_op jit(solution)/shard_map/ppermute | solution.py:211
  51.7 31.7 %collective-permute-start.6 = (f16[32,1024]{1,0:T(8,128)(2,1)S(1)}, f16[32,1024]{1,0:T(8,128)(2,1)S(1)}, u32[]{:S(2)}, u32[]{:S(2)}) collective-permute-start(f16[32,1024]{1,0:T(8,128)(2,1)S(1)} %multiply_convert_fusion.6), channel_id=1, source_target_pairs={{0,8},{1,9},{2,10},{3,11},{4,12},{5,13},{6,14},{7,15},{8,16},{9,17... | collective-permute-start | bytes 196616 | tf_op jit(solution)/shard_map/ppermute | solution.py:211
  110.3 1.1 copy-start
  154.5 2.7 %copy-start.1 = (f32[1024]{0:T(1024)S(1)}, f32[1024]{0:T(1024)}, u32[]{:S(2)}) copy-start(f32[1024]{0:T(1024)} %param.21) | copy-start | bytes 12292
  161.7 10.1 %collective-permute-start.7 = (bf16[1024,128]{1,0:T(8,128)(2,1)S(1)}, bf16[1024,128]{1,0:T(8,128)(2,1)S(1)}, u32[]{:S(2)}, u32[]{:S(2)}) collective-permute-start(bf16[1024,128]{1,0:T(8,128)(2,1)S(1)} %fusion.27), channel_id=1, source_target_pairs={{0,64},{64,128},{128,192},{192,256},{256,320},{320,384},{384,448},... | collective-permute-start | bytes 786440 | tf_op jit(solution)/shard_map/ppermute | solution.py:250
  166.7 9.5 %collective-permute-start.11 = (bf16[1024,128]{1,0:T(8,128)(2,1)S(1)}, bf16[1024,128]{1,0:T(8,128)(2,1)S(1)}, u32[]{:S(2)}, u32[]{:S(2)}) collective-permute-start(bf16[1024,128]{1,0:T(8,128)(2,1)S(1)} %fusion.19), channel_id=1, source_target_pairs={{0,448},{64,0},{128,64},{192,128},{256,192},{320,256},{384,320},{4... | collective-permute-start | bytes 786440 | tf_op jit(solution)/shard_map/ppermute | solution.py:250
  171.9 10.9 %collective-permute-start.8 = (bf16[1024,128]{1,0:T(8,128)(2,1)S(1)}, bf16[1024,128]{1,0:T(8,128)(2,1)S(1)}, u32[]{:S(2)}, u32[]{:S(2)}) collective-permute-start(bf16[1024,128]{1,0:T(8,128)(2,1)S(1)} %add_convert_fusion.5), channel_id=1, source_target_pairs={{0,64},{64,128},{128,192},{192,256},{256,320},{320,384},{384,448},... | collective-permute-start | bytes 786440 | tf_op jit(solution)/shard_map/ppermute | solution.py:250
  176.2 11.8 %collective-permute-start.12 = (bf16[1024,128]{1,0:T(8,128)(2,1)S(1)}, bf16[1024,128]{1,0:T(8,128)(2,1)S(1)}, u32[]{:S(2)}, u32[]{:S(2)}) collective-permute-start(bf16[1024,128]{1,0:T(8,128)(2,1)S(1)} %add_convert_fusion.2), channel_id=1, source_target_pairs={{0,448},{64,0},{128,64},{192,128},{256,192},{320,256},{384,320},{4... | collective-permute-start | bytes 786440 | tf_op jit(solution)/shard_map/ppermute | solution.py:250
  182.9 12.1 %collective-permute-start.9 = (bf16[1024,128]{1,0:T(8,128)(2,1)S(1)}, bf16[1024,128]{1,0:T(8,128)(2,1)S(1)}, u32[]{:S(2)}, u32[]{:S(2)}) collective-permute-start(bf16[1024,128]{1,0:T(8,128)(2,1)S(1)} %add_convert_fusion.4), channel_id=1, source_target_pairs={{0,64},{64,128},{128,192},{192,256},{256,320},{320,384},{384,448},... | collective-permute-start | bytes 786440 | tf_op jit(solution)/shard_map/ppermute | solution.py:250
  188.1 9.6 %collective-permute-start.13 = (bf16[1024,128]{1,0:T(8,128)(2,1)S(1)}, bf16[1024,128]{1,0:T(8,128)(2,1)S(1)}, u32[]{:S(2)}, u32[]{:S(2)}) collective-permute-start(bf16[1024,128]{1,0:T(8,128)(2,1)S(1)} %add_convert_fusion.1), channel_id=1, source_target_pairs={{0,448},{64,0},{128,64},{192,128},{256,192},{320,256},{384,320},{4... | collective-permute-start | bytes 786440 | tf_op jit(solution)/shard_map/ppermute | solution.py:250
  195.1 9.5 %collective-permute-start.10 = (bf16[1024,128]{1,0:T(8,128)(2,1)S(1)}, bf16[1024,128]{1,0:T(8,128)(2,1)S(1)}, u32[]{:S(2)}, u32[]{:S(2)}) collective-permute-start(bf16[1024,128]{1,0:T(8,128)(2,1)S(1)} %add_convert_fusion.3), channel_id=1, source_target_pairs={{0,64},{64,128},{128,192},{192,256},{256,320},{320,384},{384,448},... | collective-permute-start | bytes 786440 | tf_op jit(solution)/shard_map/ppermute | solution.py:250
Sparse Core Ops, SparseCore 0:
  10.7 90.9 all-gather.3

commit v5 on v2

--- a/solution.py
+++ b/solution.py
@@ -144,6 +144,7 @@
             pltpu.VMEM((count, width), jnp.float32),
             pltpu.VMEM((count, slots.shape[0] * slots.shape[1]), jnp.float32),
         ],
+        compiler_params=pltpu.CompilerParams(vmem_limit_bytes=52 << 20),
         name="attend",
     )(
         block_band,
@@ -207,20 +208,24 @@
     down_rows = whole(3)
     me = lax.axis_index("grp")
     columns = width // groups
+    way = 1 - 2 * lax.rem(lax.axis_index("tm"), 2)
 
     def term(offset):
-        owner = lax.rem(me + offset + groups, groups)
+        owner = lax.rem(me + way * offset + groups, groups)
         rows = lax.dynamic_slice_in_dim(down_rows, owner * columns, columns, 0)
-        return lax.optimization_barrier(
-            lax.dot_general(
-                hidden, rows, (((1,), (1,)), ((), ())), preferred_element_type=jnp.float32
-            )
+        value = lax.dot_general(
+            hidden, rows, (((1,), (1,)), ((), ())), preferred_element_type=jnp.float32
         )
+        return lax.optimization_barrier(value)
 
     def hop(values, by):
-        pairs = [(i, (i + by) % groups) for i in range(groups)]
+        pairs = []
+        for group in range(groups):
+            for place in range(owners):
+                target = (group + (by if place % 2 == 0 else -by)) % groups
+                pairs.append((group * owners + place, target * owners + place))
         values = values.astype(jnp.bfloat16)
-        return lax.ppermute(values, "grp", pairs)
+        return lax.ppermute(values, ("grp", "tm"), pairs)
 
     up_hops = groups // 2
     down_hops = groups - 1 - up_hops

time: 198 us -> 192 us (0.970)
  the two profiles are of different devices: /device:TPU:64 before, /device:TPU:32 now
where the time goes in v5:
time: 192 us; the launch traced here: 191 us
  blocking collectives  107 us (56%)
  starting transfers between devices  35.8 us (19%)
  waiting for transfers between devices  20.7 us (11%)
  Pallas kernels  10.6 us (6%)
  matrix products  9.46 us (5%)
  other arithmetic  6.71 us (3%)
    all_gather x1, blocking collectives, local(): gathered = lax.all_gather(shard, 'tm', axis=0, tiled=True)  77 us
    all_gather x1, blocking collectives, local(): window = lax.all_gather(sent, 'grp', axis=0, tiled=True)  29.7 us
    ppermute x7, starting transfers between devices, hop(): return lax.ppermute(values, ('grp', 'tm'), pairs)  22 us
    ppermute x7, waiting for transfers between devices, hop(): return lax.ppermute(values, ('grp', 'tm'), pairs)  20.7 us
    all_to_all x1, starting transfers between devices, local(): lax.all_to_all(payload, 'tm', split_axis=0, concat_axis=0, tiled=True)  13.8 us
    pallas_call x1, Pallas kernels, attend(): pl.pallas_call(attend_kernel, grid=(width // step,), in_specs=[pl.BlockSp...  7.87 us
    dot_general x8, matrix products, term(): lax.dot_general(hidden, rows, (((1,), (1,)), ((), ())), preferred_element...  5.74 us
    convert_element_type x1, other arithmetic, whole(): return part.astype(jnp.bfloat16).reshape(width, width)  4.2 us
  transfers between devices with their start and end apart: 8, of which 4 were waited for; matrix products, arithmetic and copies ran while one was open for 5% of the time, Pallas kernels for 0%

profile of v5, /device:TPU:32, one launch (start us, length us, event | category | flops | bytes accessed | tf_op | source)
XLA Modules:
  0.0 191.4 jit_solution(17549028659558786429)
XLA Ops:
  0.0 0.0 copy-start.4
  0.0 2.8 %pack.1 = bf16[64,8,1152]{2,1,0:T(8,128)(2,1)} custom-call(s32[1,256]{1,0:T(1,128)} %bitcast.50, s32[1,256]{1,0:T(1,128)} %bitcast.51, bf16[256,1024]{1,0:T(8,128)(2,1)} %refs_2_.1), custom_call_target="tpu_custom_call" | custom-call | tf_op jit(solution)/shard_map/pack/pallas_call | solution.py:55
  2.8 13.8 %all-to-all-start = ((bf16[64,8,1152]{2,1,0:T(8,128)(2,1)}), bf16[64,8,1152]{2,1,0:T(8,128)(2,1)S(1)}, u32[]{:S(2)}, u32[]{:S(2)}) async-start(bf16[64,8,1152]{2,1,0:T(8,128)(2,1)} %pack.1), calls=%async_computation | async-start | bytes 2359296 | tf_op jit(solution)/shard_map/all_to_all | solution.py:183
  16.6 0.0 copy-done.4
  17.3 0.0 copy-done.5
  17.4 0.0 copy-done.6
  17.4 77.0 %all-gather.2 = f16[4096,1024]{1,0:T(8,128)(2,1)S(1)} all-gather(f16[64,1024]{1,0:T(8,128)(2,1)S(1)} %multiply_convert_fusion.9), channel_id=1, replica_groups=mesh['grp'=8,'tm'=64] {'tm'}, dimensions={0}, use_global_device_ids=true | all-gather | bytes 8519680 | tf_op jit(solution)/shard_map/all_gather | solution.py:189
  94.4 4.2 %multiply_convert_fusion = (bf16[64,1,16,1024]{3,2,0,1:T(8,128)(2,1)S(1)}, bf16[64,1,16,1024]{3,2,0,1:T(8,128)(2,1)}, bf16[64,1,16,1024]{3,2,0,1:T(8,128)(2,1)}, bf16[64,1,16,1024]{3,2,0,1:T(8,128)(2,1)}) fusion(f16[64,4,16,1024]{3,2,1,0:T(8,128)(2,1)S(1)} %bitcast.37), kind=kLoop, calls=%fused_computation.9 | loop fusion | flops 12582912 | bytes 16777216 | tf_op jit(solution)/shard_map/convert_element_type | solution.py:194
  98.6 0.0 all-to-all-done.slots_ref
  98.6 0.0 copy-done
  98.6 0.0 copy-done.1
  98.6 0.0 copy-done.2
  98.6 7.9 %attend.1 = bf16[128,1024]{1,0:T(8,128)(2,1)S(1)} custom-call(s32[1]{0:T(128)S(6)} %copy.21.band_ref, bf16[64,8,1152]{2,1,0:T(8,128)(2,1)S(1)} %all-to-all-done.slots_ref, bf16[128,1024]{1,0:T(8,128)(2,1)S(1)} %copy-done, bf16[128,1024]{1,0:T(8,128)(2,1)S(1)} %copy-done, bf16[1024,1024]{1,0:T(8,128)(2,1)} %bitcast.39, bf16[1024,1024]{1,0:T(8,128)(2,1)} %bitcast.38, ...), custom_call_target="tpu_custom_call" | custom-call | tf_op jit(solution)/shard_map/attend/pallas_call | solution.py:127
  106.5 0.1 multiply_convert_fusion.8
  106.6 29.7 %all-gather.3 = f16[1024,1024]{1,0:T(8,128)(2,1)S(1)} all-gather(f16[128,1024]{1,0:T(8,128)(2,1)S(1)} %multiply_convert_fusion.8), channel_id=1, replica_groups=mesh['grp'=8,'tm'=64] {'grp'}, dimensions={0}, use_global_device_ids=true | all-gather | bytes 2359296 | tf_op jit(solution)/shard_map/all_gather | solution.py:200
  136.3 0.5 fusion.9
  136.8 0.8 multiply_reduce_fusion
  137.6 0.3 copy-done.3
  137.9 0.0 copy-done.7
  137.9 3.7 %fusion.7 = bf16[1024,1024]{1,0:T(8,128)(2,1)S(1)} fusion(bf16[1024,1024]{1,0:T(8,128)(2,1)S(1)} %bitcast.48, f16[1024,1024]{1,0:T(8,128)(2,1)S(1)} %all-gather.3, f32[1024]{0:T(1024)S(1)} %copy-done.7, f32[1024]{0:T(1024)S(1)} %add_rsqrt_fusion, f32[1024]{0:T(1024)S(1)} %broadcast_multiply_fusion), kind=kOutput, calls=%fused_computation.8 | convolution fusion | flops 2163212288 | bytes 6303744 | tf_op jit(solution)/shard_map/dot_general | solution.py:205
  141.6 0.7 fusion.15
  142.4 0.7 fusion.19
  143.1 3.3 %collective-permute-start.4 = (bf16[1024,128]{1,0:T(8,128)(2,1)S(1)}, bf16[1024,128]{1,0:T(8,128)(2,1)S(1)}, u32[]{:S(2)}, u32[]{:S(2)}) collective-permute-start(bf16[1024,128]{1,0:T(8,128)(2,1)S(1)} %fusion.19), channel_id=1, source_target_pairs={{0,448},{1,65},{2,450},{3,67},{4,452},{5,69},{6,454},{7,71},{8,456... | collective-permute-start | bytes 786440 | tf_op jit(solution)/shard_map/ppermute | solution.py:228
  146.4 0.7 fusion.25
  147.1 0.7 fusion.27
  147.9 2.7 %collective-permute-start = (bf16[1024,128]{1,0:T(8,128)(2,1)S(1)}, bf16[1024,128]{1,0:T(8,128)(2,1)S(1)}, u32[]{:S(2)}, u32[]{:S(2)}) collective-permute-start(bf16[1024,128]{1,0:T(8,128)(2,1)S(1)} %fusion.27), channel_id=1, source_target_pairs={{0,64},{1,449},{2,66},{3,451},{4,68},{5,453},{6,70},{7,455},{8,72}... | collective-permute-start | bytes 786440 | tf_op jit(solution)/shard_map/ppermute | solution.py:228
  150.6 0.7 fusion.17
  151.3 6.1 %collective-permute-done = bf16[1024,128]{1,0:T(8,128)(2,1)S(1)} collective-permute-done((bf16[1024,128]{1,0:T(8,128)(2,1)S(1)}, bf16[1024,128]{1,0:T(8,128)(2,1)S(1)}, u32[]{:S(2)}, u32[]{:S(2)}) %collective-permute-start) | collective-permute-done | bytes 262176 | tf_op jit(solution)/shard_map/ppermute | solution.py:228
  157.3 0.1 add_convert_fusion.5
  157.4 1.9 %collective-permute-start.1 = (bf16[1024,128]{1,0:T(8,128)(2,1)S(1)}, bf16[1024,128]{1,0:T(8,128)(2,1)S(1)}, u32[]{:S(2)}, u32[]{:S(2)}) collective-permute-start(bf16[1024,128]{1,0:T(8,128)(2,1)S(1)} %add_convert_fusion.5), channel_id=1, source_target_pairs={{0,64},{1,449},{2,66},{3,451},{4,68},{5,453},{6,70},{7,455},{8,72}... | collective-permute-start | bytes 786440 | tf_op jit(solution)/shard_map/ppermute | solution.py:228
  159.3 0.7 fusion.23
  160.1 0.0 collective-permute-done.4
  160.1 0.1 add_convert_fusion.2
  160.1 5.1 %collective-permute-start.5 = (bf16[1024,128]{1,0:T(8,128)(2,1)S(1)}, bf16[1024,128]{1,0:T(8,128)(2,1)S(1)}, u32[]{:S(2)}, u32[]{:S(2)}) collective-permute-start(bf16[1024,128]{1,0:T(8,128)(2,1)S(1)} %add_convert_fusion.2), channel_id=1, source_target_pairs={{0,448},{1,65},{2,450},{3,67},{4,452},{5,69},{6,454},{7,71},{8,456... | collective-permute-start | bytes 786440 | tf_op jit(solution)/shard_map/ppermute | solution.py:228
  165.3 4.3 %collective-permute-done.1 = bf16[1024,128]{1,0:T(8,128)(2,1)S(1)} collective-permute-done((bf16[1024,128]{1,0:T(8,128)(2,1)S(1)}, bf16[1024,128]{1,0:T(8,128)(2,1)S(1)}, u32[]{:S(2)}, u32[]{:S(2)}) %collective-permute-start.1) | collective-permute-done | bytes 262176 | tf_op jit(solution)/shard_map/ppermute | solution.py:228
  169.5 0.1 add_convert_fusion.4
  169.6 1.9 %collective-permute-start.2 = (bf16[1024,128]{1,0:T(8,128)(2,1)S(1)}, bf16[1024,128]{1,0:T(8,128)(2,1)S(1)}, u32[]{:S(2)}, u32[]{:S(2)}) collective-permute-start(bf16[1024,128]{1,0:T(8,128)(2,1)S(1)} %add_convert_fusion.4), channel_id=1, source_target_pairs={{0,64},{1,449},{2,66},{3,451},{4,68},{5,453},{6,70},{7,455},{8,72}... | collective-permute-start | bytes 786440 | tf_op jit(solution)/shard_map/ppermute | solution.py:228
  171.5 0.7 fusion.21
  172.2 0.0 collective-permute-done.5
  172.2 0.1 add_convert_fusion.1
  172.3 5.1 %collective-permute-start.6 = (bf16[1024,128]{1,0:T(8,128)(2,1)S(1)}, bf16[1024,128]{1,0:T(8,128)(2,1)S(1)}, u32[]{:S(2)}, u32[]{:S(2)}) collective-permute-start(bf16[1024,128]{1,0:T(8,128)(2,1)S(1)} %add_convert_fusion.1), channel_id=1, source_target_pairs={{0,448},{1,65},{2,450},{3,67},{4,452},{5,69},{6,454},{7,71},{8,456... | collective-permute-start | bytes 786440 | tf_op jit(solution)/shard_map/ppermute | solution.py:228
  177.4 3.6 %collective-permute-done.2 = bf16[1024,128]{1,0:T(8,128)(2,1)S(1)} collective-permute-done((bf16[1024,128]{1,0:T(8,128)(2,1)S(1)}, bf16[1024,128]{1,0:T(8,128)(2,1)S(1)}, u32[]{:S(2)}, u32[]{:S(2)}) %collective-permute-start.2) | collective-permute-done | bytes 262176 | tf_op jit(solution)/shard_map/ppermute | solution.py:228
  181.0 0.1 add_convert_fusion.3
  181.1 1.9 %collective-permute-start.3 = (bf16[1024,128]{1,0:T(8,128)(2,1)S(1)}, bf16[1024,128]{1,0:T(8,128)(2,1)S(1)}, u32[]{:S(2)}, u32[]{:S(2)}) collective-permute-start(bf16[1024,128]{1,0:T(8,128)(2,1)S(1)} %add_convert_fusion.3), channel_id=1, source_target_pairs={{0,64},{1,449},{2,66},{3,451},{4,68},{5,453},{6,70},{7,455},{8,72}... | collective-permute-start | bytes 786440 | tf_op jit(solution)/shard_map/ppermute | solution.py:228
  183.0 0.7 fusion.29
  183.7 0.0 collective-permute-done.6
  183.7 6.8 %collective-permute-done.3 = bf16[1024,128]{1,0:T(8,128)(2,1)S(1)} collective-permute-done((bf16[1024,128]{1,0:T(8,128)(2,1)S(1)}, bf16[1024,128]{1,0:T(8,128)(2,1)S(1)}, u32[]{:S(2)}, u32[]{:S(2)}) %collective-permute-start.3) | collective-permute-done | bytes 262176 | tf_op jit(solution)/shard_map/ppermute | solution.py:228
  190.5 0.9 add_convert_fusion
  (11 shorter events, 0.1 us)
Async XLA Ops:
  0.0 16.6 %copy-start.4 = (bf16[16,2048]{1,0:T(8,128)(2,1)S(1)}, bf16[16,2048]{1,0:T(8,128)(2,1)}, u32[]{:S(2)}) copy-start(bf16[16,2048]{1,0:T(8,128)(2,1)} %param.17) | copy-start | bytes 196612
  0.0 17.3 %copy-start.5 = (bf16[1024,16]{0,1:T(8,128)(2,1)S(1)}, bf16[1024,16]{0,1:T(8,128)(2,1)}, u32[]{:S(2)}) copy-start(bf16[1024,16]{0,1:T(8,128)(2,1)} %param.23) | copy-start | bytes 98308
  0.0 17.4 %copy-start.6 = (bf16[16,1024]{1,0:T(8,128)(2,1)S(1)}, bf16[16,1024]{1,0:T(8,128)(2,1)}, u32[]{:S(2)}) copy-start(bf16[16,1024]{1,0:T(8,128)(2,1)} %param.22) | copy-start | bytes 98308
  2.8 95.8 %all-to-all-start = ((bf16[64,8,1152]{2,1,0:T(8,128)(2,1)}), bf16[64,8,1152]{2,1,0:T(8,128)(2,1)S(1)}, u32[]{:S(2)}, u32[]{:S(2)}) async-start(bf16[64,8,1152]{2,1,0:T(8,128)(2,1)} %pack.1), calls=%async_computation | async-start | bytes 2359296 | tf_op jit(solution)/shard_map/all_to_all | solution.py:183
  94.4 4.2 %copy-start = (bf16[128,1024]{1,0:T(8,128)(2,1)S(1)}, bf16[128,1024]{1,0:T(8,128)(2,1)}, u32[]{:S(2)}) copy-start(bf16[128,1024]{1,0:T(8,128)(2,1)} %query_ref.1) | copy-start | bytes 786436
  94.4 4.2 %copy-start.1 = (f32[1024]{0:T(1024)S(1)}, f32[1024]{0:T(1024)}, u32[]{:S(2)}) copy-start(f32[1024]{0:T(1024)} %param.18) | copy-start | bytes 12292
  94.4 4.2 %copy-start.2 = (f32[1024]{0:T(1024)S(1)}, f32[1024]{0:T(1024)}, u32[]{:S(2)}) copy-start(f32[1024]{0:T(1024)} %param.19) | copy-start | bytes 12292
  136.3 1.6 copy-start.3
  136.3 1.6 copy-start.7
  143.1 17.0 %collective-permute-start.4 = (bf16[1024,128]{1,0:T(8,128)(2,1)S(1)}, bf16[1024,128]{1,0:T(8,128)(2,1)S(1)}, u32[]{:S(2)}, u32[]{:S(2)}) collective-permute-start(bf16[1024,128]{1,0:T(8,128)(2,1)S(1)} %fusion.19), channel_id=1, source_target_pairs={{0,448},{1,65},{2,450},{3,67},{4,452},{5,69},{6,454},{7,71},{8,456... | collective-permute-start | bytes 786440 | tf_op jit(solution)/shard_map/ppermute | solution.py:228
  147.9 9.5 %collective-permute-start = (bf16[1024,128]{1,0:T(8,128)(2,1)S(1)}, bf16[1024,128]{1,0:T(8,128)(2,1)S(1)}, u32[]{:S(2)}, u32[]{:S(2)}) collective-permute-start(bf16[1024,128]{1,0:T(8,128)(2,1)S(1)} %fusion.27), channel_id=1, source_target_pairs={{0,64},{1,449},{2,66},{3,451},{4,68},{5,453},{6,70},{7,455},{8,72}... | collective-permute-start | bytes 786440 | tf_op jit(solution)/shard_map/ppermute | solution.py:228
  157.4 12.1 %collective-permute-start.1 = (bf16[1024,128]{1,0:T(8,128)(2,1)S(1)}, bf16[1024,128]{1,0:T(8,128)(2,1)S(1)}, u32[]{:S(2)}, u32[]{:S(2)}) collective-permute-start(bf16[1024,128]{1,0:T(8,128)(2,1)S(1)} %add_convert_fusion.5), channel_id=1, source_target_pairs={{0,64},{1,449},{2,66},{3,451},{4,68},{5,453},{6,70},{7,455},{8,72}... | collective-permute-start | bytes 786440 | tf_op jit(solution)/shard_map/ppermute | solution.py:228
  160.1 12.1 %collective-permute-start.5 = (bf16[1024,128]{1,0:T(8,128)(2,1)S(1)}, bf16[1024,128]{1,0:T(8,128)(2,1)S(1)}, u32[]{:S(2)}, u32[]{:S(2)}) collective-permute-start(bf16[1024,128]{1,0:T(8,128)(2,1)S(1)} %add_convert_fusion.2), channel_id=1, source_target_pairs={{0,448},{1,65},{2,450},{3,67},{4,452},{5,69},{6,454},{7,71},{8,456... | collective-permute-start | bytes 786440 | tf_op jit(solution)/shard_map/ppermute | solution.py:228
  169.6 11.4 %collective-permute-start.2 = (bf16[1024,128]{1,0:T(8,128)(2,1)S(1)}, bf16[1024,128]{1,0:T(8,128)(2,1)S(1)}, u32[]{:S(2)}, u32[]{:S(2)}) collective-permute-start(bf16[1024,128]{1,0:T(8,128)(2,1)S(1)} %add_convert_fusion.4), channel_id=1, source_target_pairs={{0,64},{1,449},{2,66},{3,451},{4,68},{5,453},{6,70},{7,455},{8,72}... | collective-permute-start | bytes 786440 | tf_op jit(solution)/shard_map/ppermute | solution.py:228
  172.3 11.4 %collective-permute-start.6 = (bf16[1024,128]{1,0:T(8,128)(2,1)S(1)}, bf16[1024,128]{1,0:T(8,128)(2,1)S(1)}, u32[]{:S(2)}, u32[]{:S(2)}) collective-permute-start(bf16[1024,128]{1,0:T(8,128)(2,1)S(1)} %add_convert_fusion.1), channel_id=1, source_target_pairs={{0,448},{1,65},{2,450},{3,67},{4,452},{5,69},{6,454},{7,71},{8,456... | collective-permute-start | bytes 786440 | tf_op jit(solution)/shard_map/ppermute | solution.py:228
  181.1 9.5 %collective-permute-start.3 = (bf16[1024,128]{1,0:T(8,128)(2,1)S(1)}, bf16[1024,128]{1,0:T(8,128)(2,1)S(1)}, u32[]{:S(2)}, u32[]{:S(2)}) collective-permute-start(bf16[1024,128]{1,0:T(8,128)(2,1)S(1)} %add_convert_fusion.3), channel_id=1, source_target_pairs={{0,64},{1,449},{2,66},{3,451},{4,68},{5,453},{6,70},{7,455},{8,72}... | collective-permute-start | bytes 786440 | tf_op jit(solution)/shard_map/ppermute | solution.py:228

commit v6 on v2

--- a/solution.py
+++ b/solution.py
@@ -144,6 +144,7 @@
             pltpu.VMEM((count, width), jnp.float32),
             pltpu.VMEM((count, slots.shape[0] * slots.shape[1]), jnp.float32),
         ],
+        compiler_params=pltpu.CompilerParams(vmem_limit_bytes=49 << 20),
         name="attend",
     )(
         block_band,
@@ -211,11 +212,10 @@
     def term(offset):
         owner = lax.rem(me + offset + groups, groups)
         rows = lax.dynamic_slice_in_dim(down_rows, owner * columns, columns, 0)
-        return lax.optimization_barrier(
-            lax.dot_general(
-                hidden, rows, (((1,), (1,)), ((), ())), preferred_element_type=jnp.float32
-            )
+        value = lax.dot_general(
+            hidden, rows, (((1,), (1,)), ((), ())), preferred_element_type=jnp.float32
         )
+        return lax.optimization_barrier(value)
 
     def hop(values, by):
         pairs = [(i, (i + by) % groups) for i in range(groups)]

time: 198 us -> 195 us (0.985)
  transfers between devices with their start and end apart: 8 -> 8, of which waited for: 4 -> 4; matrix products, arithmetic and copies ran while one was open for 4% -> 5% of each run, Pallas kernels for 0% -> 0%
where the time goes in v6:
time: 195 us; the launch traced here: 194 us
  blocking collectives  109 us (56%)
  starting transfers between devices  35.6 us (18%)
  waiting for transfers between devices  21.7 us (11%)
  Pallas kernels  10.4 us (5%)
  matrix products  9.43 us (5%)
  other arithmetic  6.71 us (3%)
    all_gather x1, blocking collectives, local(): gathered = lax.all_gather(shard, 'tm', axis=0, tiled=True)  77.4 us
    all_gather x1, blocking collectives, local(): window = lax.all_gather(sent, 'grp', axis=0, tiled=True)  31.7 us
    ppermute x7, starting transfers between devices, hop(): return lax.ppermute(values, 'grp', pairs)  22.6 us
    ppermute x7, waiting for transfers between devices, hop(): return lax.ppermute(values, 'grp', pairs)  21.7 us
    all_to_all x1, starting transfers between devices, local(): lax.all_to_all(payload, 'tm', split_axis=0, concat_axis=0, tiled=True)  13 us
    pallas_call x1, Pallas kernels, attend(): pl.pallas_call(attend_kernel, grid=(width // step,), in_specs=[pl.BlockSp...  7.61 us
    dot_general x8, matrix products, term(): lax.dot_general(hidden, rows, (((1,), (1,)), ((), ())), preferred_element...  5.72 us
    convert_element_type x1, other arithmetic, whole(): return part.astype(jnp.bfloat16).reshape(width, width)  4.21 us
  transfers between devices with their start and end apart: 8, of which 4 were waited for; matrix products, arithmetic and copies ran while one was open for 5% of the time, Pallas kernels for 0%

profile of v6, /device:TPU:64, one launch (start us, length us, event | category | flops | bytes accessed | tf_op | source)
XLA Modules:
  0.0 194.2 jit_solution(8048215319943006721)
XLA Ops:
  0.0 2.8 %pack.1 = bf16[64,8,1152]{2,1,0:T(8,128)(2,1)} custom-call(s32[1,256]{1,0:T(1,128)} %bitcast.50, s32[1,256]{1,0:T(1,128)} %bitcast.51, bf16[256,1024]{1,0:T(8,128)(2,1)} %refs_2_.1), custom_call_target="tpu_custom_call" | custom-call | tf_op jit(solution)/shard_map/pack/pallas_call | solution.py:55
  2.8 13.0 %all-to-all-start = ((bf16[64,8,1152]{2,1,0:T(8,128)(2,1)}), bf16[64,8,1152]{2,1,0:T(8,128)(2,1)S(1)}, u32[]{:S(2)}, u32[]{:S(2)}) async-start(bf16[64,8,1152]{2,1,0:T(8,128)(2,1)} %pack.1), calls=%async_computation | async-start | bytes 2359296 | tf_op jit(solution)/shard_map/all_to_all | solution.py:183
  15.8 0.0 copy-done.5
  16.5 0.0 copy-done.6
  16.5 0.0 copy-done.7
  16.6 77.4 %all-gather.2 = f16[4096,1024]{1,0:T(8,128)(2,1)S(1)} all-gather(f16[64,1024]{1,0:T(8,128)(2,1)S(1)} %multiply_convert_fusion.9), channel_id=1, replica_groups=mesh['grp'=8,'tm'=64] {'tm'}, dimensions={0}, use_global_device_ids=true | all-gather | bytes 8519680 | tf_op jit(solution)/shard_map/all_gather | solution.py:189
  94.0 4.2 %multiply_convert_fusion = (bf16[64,1,16,1024]{3,2,0,1:T(8,128)(2,1)}, bf16[64,1,16,1024]{3,2,0,1:T(8,128)(2,1)}, bf16[64,1,16,1024]{3,2,0,1:T(8,128)(2,1)}, bf16[64,1,16,1024]{3,2,0,1:T(8,128)(2,1)S(1)}) fusion(f16[64,4,16,1024]{3,2,1,0:T(8,128)(2,1)S(1)} %bitcast.38), kind=kLoop, calls=%fused_computation.9 | loop fusion | flops 12582912 | bytes 16777216 | tf_op jit(solution)/shard_map/convert_element_type | solution.py:194
  98.2 0.0 all-to-all-done.slots_ref
  98.2 0.0 copy-done
  98.2 0.0 copy-done.1
  98.3 0.0 copy-done.2
  98.3 7.6 %attend.1 = bf16[128,1024]{1,0:T(8,128)(2,1)S(1)} custom-call(s32[1]{0:T(128)S(6)} %copy.21.band_ref, bf16[64,8,1152]{2,1,0:T(8,128)(2,1)S(1)} %all-to-all-done.slots_ref, bf16[128,1024]{1,0:T(8,128)(2,1)S(1)} %copy-done, bf16[128,1024]{1,0:T(8,128)(2,1)S(1)} %copy-done, bf16[1024,1024]{1,0:T(8,128)(2,1)S(1)} %bitcast.35, bf16[1024,1024]{1,0:T(8,128)(2,1)} %bitcast.39, ...), custom_call_target="tpu_custom_call" | custom-call | tf_op jit(solution)/shard_map/attend/pallas_call | solution.py:127
  105.9 0.1 multiply_convert_fusion.8
  106.0 31.7 %all-gather.3 = f16[1024,1024]{1,0:T(8,128)(2,1)S(1)} all-gather(f16[128,1024]{1,0:T(8,128)(2,1)S(1)} %multiply_convert_fusion.8), channel_id=1, replica_groups=mesh['grp'=8,'tm'=64] {'grp'}, dimensions={0}, use_global_device_ids=true | all-gather | bytes 2359296 | tf_op jit(solution)/shard_map/all_gather | solution.py:200
  137.6 0.5 fusion.9
  138.1 0.8 multiply_reduce_fusion
  138.9 0.3 copy-done.4
  139.2 0.0 copy-done.8
  139.2 3.7 %fusion.7 = bf16[1024,1024]{1,0:T(8,128)(2,1)S(1)} fusion(bf16[1024,1024]{1,0:T(8,128)(2,1)S(1)} %bitcast.48, f16[1024,1024]{1,0:T(8,128)(2,1)S(1)} %all-gather.3, f32[1024]{0:T(1024)S(1)} %copy-done.8, f32[1024]{0:T(1024)S(1)} %add_rsqrt_fusion, f32[1024]{0:T(1024)S(1)} %broadcast_multiply_fusion), kind=kOutput, calls=%fused_computation.8 | convolution fusion | flops 2163212288 | bytes 6303744 | tf_op jit(solution)/shard_map/dot_general | solution.py:205
  142.9 0.0 copy-done.3
  143.0 0.7 fusion.15
  143.7 0.7 fusion.19
  144.4 4.4 %collective-permute-start.4 = (bf16[1024,128]{1,0:T(8,128)(2,1)S(1)}, bf16[1024,128]{1,0:T(8,128)(2,1)S(1)}, u32[]{:S(2)}, u32[]{:S(2)}) collective-permute-start(bf16[1024,128]{1,0:T(8,128)(2,1)S(1)} %fusion.19), channel_id=1, source_target_pairs={{0,448},{64,0},{128,64},{192,128},{256,192},{320,256},{384,320},{4... | collective-permute-start | bytes 786440 | tf_op jit(solution)/shard_map/ppermute | solution.py:223
  148.8 0.7 fusion.25
  149.5 0.7 fusion.27
  150.2 1.9 collective-permute-start
  152.1 0.7 fusion.17
  152.9 7.4 %collective-permute-done = bf16[1024,128]{1,0:T(8,128)(2,1)S(1)} collective-permute-done((bf16[1024,128]{1,0:T(8,128)(2,1)S(1)}, bf16[1024,128]{1,0:T(8,128)(2,1)S(1)}, u32[]{:S(2)}, u32[]{:S(2)}) %collective-permute-start) | collective-permute-done | bytes 262176 | tf_op jit(solution)/shard_map/ppermute | solution.py:223
  160.3 0.1 add_convert_fusion.5
  160.4 1.9 collective-permute-start.1
  162.3 0.7 fusion.23
  163.0 0.0 collective-permute-done.4
  163.0 0.1 add_convert_fusion.2
  163.1 5.1 %collective-permute-start.5 = (bf16[1024,128]{1,0:T(8,128)(2,1)S(1)}, bf16[1024,128]{1,0:T(8,128)(2,1)S(1)}, u32[]{:S(2)}, u32[]{:S(2)}) collective-permute-start(bf16[1024,128]{1,0:T(8,128)(2,1)S(1)} %add_convert_fusion.2), channel_id=1, source_target_pairs={{0,448},{64,0},{128,64},{192,128},{256,192},{320,256},{384,320},{4... | collective-permute-start | bytes 786440 | tf_op jit(solution)/shard_map/ppermute | solution.py:223
  168.2 3.4 %collective-permute-done.1 = bf16[1024,128]{1,0:T(8,128)(2,1)S(1)} collective-permute-done((bf16[1024,128]{1,0:T(8,128)(2,1)S(1)}, bf16[1024,128]{1,0:T(8,128)(2,1)S(1)}, u32[]{:S(2)}, u32[]{:S(2)}) %collective-permute-start.1) | collective-permute-done | bytes 262176 | tf_op jit(solution)/shard_map/ppermute | solution.py:223
  171.6 0.1 add_convert_fusion.4
  171.7 1.9 collective-permute-start.2
  173.6 0.7 fusion.21
  174.3 0.0 collective-permute-done.5
  174.3 0.1 add_convert_fusion.1
  174.4 5.4 %collective-permute-start.6 = (bf16[1024,128]{1,0:T(8,128)(2,1)S(1)}, bf16[1024,128]{1,0:T(8,128)(2,1)S(1)}, u32[]{:S(2)}, u32[]{:S(2)}) collective-permute-start(bf16[1024,128]{1,0:T(8,128)(2,1)S(1)} %add_convert_fusion.1), channel_id=1, source_target_pairs={{0,448},{64,0},{128,64},{192,128},{256,192},{320,256},{384,320},{4... | collective-permute-start | bytes 786440 | tf_op jit(solution)/shard_map/ppermute | solution.py:223
  179.8 4.0 %collective-permute-done.2 = bf16[1024,128]{1,0:T(8,128)(2,1)S(1)} collective-permute-done((bf16[1024,128]{1,0:T(8,128)(2,1)S(1)}, bf16[1024,128]{1,0:T(8,128)(2,1)S(1)}, u32[]{:S(2)}, u32[]{:S(2)}) %collective-permute-start.2) | collective-permute-done | bytes 262176 | tf_op jit(solution)/shard_map/ppermute | solution.py:223
  183.8 0.1 add_convert_fusion.3
  183.9 1.9 collective-permute-start.3
  185.8 0.7 fusion.29
  186.5 0.0 collective-permute-done.6
  186.6 6.8 %collective-permute-done.3 = bf16[1024,128]{1,0:T(8,128)(2,1)S(1)} collective-permute-done((bf16[1024,128]{1,0:T(8,128)(2,1)S(1)}, bf16[1024,128]{1,0:T(8,128)(2,1)S(1)}, u32[]{:S(2)}, u32[]{:S(2)}) %collective-permute-start.3) | collective-permute-done | bytes 262176 | tf_op jit(solution)/shard_map/ppermute | solution.py:223
  193.4 0.9 add_convert_fusion
  (13 shorter events, 0.1 us)
Async XLA Ops:
  0.0 15.8 %copy-start.5 = (bf16[16,2048]{1,0:T(8,128)(2,1)S(1)}, bf16[16,2048]{1,0:T(8,128)(2,1)}, u32[]{:S(2)}) copy-start(bf16[16,2048]{1,0:T(8,128)(2,1)} %param.17) | copy-start | bytes 196612
  0.0 16.5 %copy-start.6 = (bf16[1024,16]{0,1:T(8,128)(2,1)S(1)}, bf16[1024,16]{0,1:T(8,128)(2,1)}, u32[]{:S(2)}) copy-start(bf16[1024,16]{0,1:T(8,128)(2,1)} %param.23) | copy-start | bytes 98308
  0.0 16.5 %copy-start.7 = (bf16[16,1024]{1,0:T(8,128)(2,1)S(1)}, bf16[16,1024]{1,0:T(8,128)(2,1)}, u32[]{:S(2)}) copy-start(bf16[16,1024]{1,0:T(8,128)(2,1)} %param.22) | copy-start | bytes 98308
  2.8 95.5 %all-to-all-start = ((bf16[64,8,1152]{2,1,0:T(8,128)(2,1)}), bf16[64,8,1152]{2,1,0:T(8,128)(2,1)S(1)}, u32[]{:S(2)}, u32[]{:S(2)}) async-start(bf16[64,8,1152]{2,1,0:T(8,128)(2,1)} %pack.1), calls=%async_computation | async-start | bytes 2359296 | tf_op jit(solution)/shard_map/all_to_all | solution.py:183
  94.0 4.2 %copy-start = (bf16[128,1024]{1,0:T(8,128)(2,1)S(1)}, bf16[128,1024]{1,0:T(8,128)(2,1)}, u32[]{:S(2)}) copy-start(bf16[128,1024]{1,0:T(8,128)(2,1)} %query_ref.1) | copy-start | bytes 786436
  94.0 4.2 %copy-start.1 = (f32[1024]{0:T(1024)S(1)}, f32[1024]{0:T(1024)}, u32[]{:S(2)}) copy-start(f32[1024]{0:T(1024)} %param.18) | copy-start | bytes 12292
  94.0 4.2 %copy-start.2 = (f32[1024]{0:T(1024)S(1)}, f32[1024]{0:T(1024)}, u32[]{:S(2)}) copy-start(f32[1024]{0:T(1024)} %param.19) | copy-start | bytes 12292
  137.6 1.6 copy-start.4
  137.6 1.6 copy-start.8
  139.2 3.7 %copy-start.3 = (bf16[64,1,16,1024]{3,2,0,1:T(8,128)(2,1)S(1)}, bf16[64,1,16,1024]{3,2,0,1:T(8,128)(2,1)}, u32[]{:S(2)}) copy-start(bf16[64,1,16,1024]{3,2,0,1:T(8,128)(2,1)} %get-tuple-element.5) | copy-start | bytes 6291460
  144.4 18.6 %collective-permute-start.4 = (bf16[1024,128]{1,0:T(8,128)(2,1)S(1)}, bf16[1024,128]{1,0:T(8,128)(2,1)S(1)}, u32[]{:S(2)}, u32[]{:S(2)}) collective-permute-start(bf16[1024,128]{1,0:T(8,128)(2,1)S(1)} %fusion.19), channel_id=1, source_target_pairs={{0,448},{64,0},{128,64},{192,128},{256,192},{320,256},{384,320},{4... | collective-permute-start | bytes 786440 | tf_op jit(solution)/shard_map/ppermute | solution.py:223
  150.2 10.1 %collective-permute-start = (bf16[1024,128]{1,0:T(8,128)(2,1)S(1)}, bf16[1024,128]{1,0:T(8,128)(2,1)S(1)}, u32[]{:S(2)}, u32[]{:S(2)}) collective-permute-start(bf16[1024,128]{1,0:T(8,128)(2,1)S(1)} %fusion.27), channel_id=1, source_target_pairs={{0,64},{64,128},{128,192},{192,256},{256,320},{320,384},{384,448},... | collective-permute-start | bytes 786440 | tf_op jit(solution)/shard_map/ppermute | solution.py:223
  160.4 11.2 %collective-permute-start.1 = (bf16[1024,128]{1,0:T(8,128)(2,1)S(1)}, bf16[1024,128]{1,0:T(8,128)(2,1)S(1)}, u32[]{:S(2)}, u32[]{:S(2)}) collective-permute-start(bf16[1024,128]{1,0:T(8,128)(2,1)S(1)} %add_convert_fusion.5), channel_id=1, source_target_pairs={{0,64},{64,128},{128,192},{192,256},{256,320},{320,384},{384,448},... | collective-permute-start | bytes 786440 | tf_op jit(solution)/shard_map/ppermute | solution.py:223
  163.1 11.2 %collective-permute-start.5 = (bf16[1024,128]{1,0:T(8,128)(2,1)S(1)}, bf16[1024,128]{1,0:T(8,128)(2,1)S(1)}, u32[]{:S(2)}, u32[]{:S(2)}) collective-permute-start(bf16[1024,128]{1,0:T(8,128)(2,1)S(1)} %add_convert_fusion.2), channel_id=1, source_target_pairs={{0,448},{64,0},{128,64},{192,128},{256,192},{320,256},{384,320},{4... | collective-permute-start | bytes 786440 | tf_op jit(solution)/shard_map/ppermute | solution.py:223
  171.7 12.2 %collective-permute-start.2 = (bf16[1024,128]{1,0:T(8,128)(2,1)S(1)}, bf16[1024,128]{1,0:T(8,128)(2,1)S(1)}, u32[]{:S(2)}, u32[]{:S(2)}) collective-permute-start(bf16[1024,128]{1,0:T(8,128)(2,1)S(1)} %add_convert_fusion.4), channel_id=1, source_target_pairs={{0,64},{64,128},{128,192},{192,256},{256,320},{320,384},{384,448},... | collective-permute-start | bytes 786440 | tf_op jit(solution)/shard_map/ppermute | solution.py:223
  174.4 12.2 %collective-permute-start.6 = (bf16[1024,128]{1,0:T(8,128)(2,1)S(1)}, bf16[1024,128]{1,0:T(8,128)(2,1)S(1)}, u32[]{:S(2)}, u32[]{:S(2)}) collective-permute-start(bf16[1024,128]{1,0:T(8,128)(2,1)S(1)} %add_convert_fusion.1), channel_id=1, source_target_pairs={{0,448},{64,0},{128,64},{192,128},{256,192},{320,256},{384,320},{4... | collective-permute-start | bytes 786440 | tf_op jit(solution)/shard_map/ppermute | solution.py:223
  183.9 9.5 %collective-permute-start.3 = (bf16[1024,128]{1,0:T(8,128)(2,1)S(1)}, bf16[1024,128]{1,0:T(8,128)(2,1)S(1)}, u32[]{:S(2)}, u32[]{:S(2)}) collective-permute-start(bf16[1024,128]{1,0:T(8,128)(2,1)S(1)} %add_convert_fusion.3), channel_id=1, source_target_pairs={{0,64},{64,128},{128,192},{192,256},{256,320},{320,384},{384,448},... | collective-permute-start | bytes 786440 | tf_op jit(solution)/shard_map/ppermute | solution.py:223
